TPU v7x, 32 devices: a whole 2x2x4 slice. The times are simulated.
32 devices in a mesh: row: 4 (over y, x), col: 8 (over z, core).
Axes of the slice: x: 2, y: 2, z: 4, core: 2. Of those that a mesh axis runs over, the one named last changes fastest.
Arguments:
- scalar_field: float32 [256, 256, 1024], P('col', 'row'), may hold values from -1.2 to 1.2
- reaction: float32 [256, 256, 1024], P('col', 'row'), may hold values from 0.5 to 4
- x_faces: float32 [1024], replicated, may hold values from 0.5 to 4
- y_faces: float32 [256], replicated, may hold values from 0.5 to 4
- z_faces: float32 [256], replicated, may hold values from 0.5 to 4
- x_inverse: float32 [8, 128, 128], replicated, may hold values from 0 to 1, as said below
- y_inverse: float32 [2, 128, 128], replicated, may hold values from 0 to 1, as said below
- z_inverse: float32 [2, 128, 128], replicated, may hold values from 0 to 1, as said below
Outputs:
- advanced: float32 [256, 256, 1024], P('col', 'row')
Inputs may be any that keep to these rules, and one draw needn't show every extreme that they name: x_inverse[c] is, up to float32 rounding, the inverse of the block of rows and columns c * 128 to (c + 1) * 128 - 1 of the matrix I - 500 A_x along one x line. y_inverse[c] is, up to float32 rounding, the inverse of the block of rows and columns c * 128 to (c + 1) * 128 - 1 of the matrix I - 500 A_y along one y line. z_inverse[c] is, up to float32 rounding, the inverse of the block of rows and columns c * 128 to (c + 1) * 128 - 1 of the matrix I - 500 A_z along one z line.
All inputs are finite; a program needn't handle non-finite values.
Results may differ from a plain program's by a relative error of at most 0.0003.
Values sent between devices are 32-bit elements; how exact they have to be, the bound alone decides.
A program may use at most 128 MiB of HBM per device.

v0:
```python
import functools

import jax
import jax.numpy as jnp
from jax import lax
from jax.experimental import pallas as pl
from jax.experimental.pallas import tpu as pltpu
from jax.sharding import PartitionSpec as P

WEIGHT = 0.5
STEP = 1000.0
MESH = pl.DeviceIdType.MESH
VMEM_LIMIT = 24 * 1024 * 1024


def shifted(a, by, fill):
    n = a.shape[1]
    lane = lax.broadcasted_iota(jnp.int32, a.shape, 1)
    if by > 0:
        return jnp.where(lane >= by, pltpu.roll(a, by, 1), fill)
    return jnp.where(lane < n + by, pltpu.roll(a, n + by, 1), fill)


def running_sum(a):
    by = 1
    while by < a.shape[1]:
        a = a + shifted(a, by, 0.0)
        by *= 2
    return a


def ladder(couple, sign):
    p00, p01, p10, p11 = 1.0 + couple, couple, jnp.ones_like(couple), couple
    by = 1
    while by < couple.shape[1]:
        q00, q01 = shifted(p00, sign * by, 1.0), shifted(p01, sign * by, 0.0)
        q10, q11 = shifted(p10, sign * by, 0.0), shifted(p11, sign * by, 1.0)
        n00, n01 = p00 * q00 + p01 * q10, p00 * q01 + p01 * q11
        n10, n11 = p10 * q00 + p11 * q10, p10 * q01 + p11 * q11
        scale = 1.0 / (n00 + n01 + n10 + n11)
        p00, p01, p10, p11 = n00 * scale, n01 * scale, n10 * scale, n11 * scale
        by *= 2
    return p00 / p10


def as_column(line, rows):
    n = line.shape[1]
    return jnp.transpose(jnp.broadcast_to(line, (n, n)))[:rows, :rows]


def block_of_inverse(diagonal, sums, n):
    i = lax.broadcasted_iota(jnp.int32, (n, n), 0)
    j = lax.broadcasted_iota(jnp.int32, (n, n), 1)
    near = jnp.where(i >= j, diagonal[:, :n], as_column(diagonal, n))
    return near * jnp.exp(-jnp.abs(as_column(sums, n) - sums[:, :n]))


def table_kernel(
    nr, nc, xf_ref, yf_ref, zf_ref, field_ref, xh_ref, xl_ref, xp_ref, ym_ref, yt_ref, zt_ref,
    held_ref, yhalo_ref, zhalo_ref, strips, edges, fetch_sem, strip_sem, send_sem, recv_sem,
):
    row, col = lax.axis_index("row"), lax.axis_index("col")
    zc, yc, _ = field_ref.shape
    tall = strips.shape[2]
    strip_copies = [
        pltpu.make_async_copy(
            field_ref.at[:, pl.ds(start, tall)], strips.at[side], strip_sem.at[side]
        )
        for side, start in ((0, yc - tall), (1, 0))
    ]
    for copy in strip_copies:
        copy.start()
    fetch = pltpu.make_async_copy(field_ref, held_ref, fetch_sem)
    fetch.start()
    places = [
        (row < nr - 1, row > 0, (row + 1, col)),
        (row > 0, row < nr - 1, (row - 1, col)),
        (col < nc - 1, col > 0, (row, col + 1)),
        (col > 0, col < nc - 1, (row, col - 1)),
    ]
    barrier = pltpu.get_barrier_semaphore()
    expected = 0
    for to, _, device in places:
        expected += to.astype(jnp.int32)

        @pl.when(to)
        def _():
            pl.semaphore_signal(barrier, inc=1, device_id=device, device_id_type=MESH)

    pl.semaphore_wait(barrier, expected)
    ends = [
        (edges.at[0], yhalo_ref.at[0]),
        (edges.at[1], yhalo_ref.at[1]),
        (field_ref.at[zc - 1], zhalo_ref.at[0]),
        (field_ref.at[0], zhalo_ref.at[1]),
    ]
    halo = [
        pltpu.make_async_remote_copy(
            src_ref=source, dst_ref=target, send_sem=send_sem.at[k], recv_sem=recv_sem.at[k],
            device_id=places[k][2], device_id_type=MESH,
        )
        for k, (source, target) in enumerate(ends)
    ]
    for k in (2, 3):
        @pl.when(places[k][0])
        def _():
            halo[k].start()

    for side in (0, 1):
        strip_copies[side].wait()
        for z in range(zc):
            at = tall - 1 if side == 0 else 0
            edges[side, z:z + 1] = strips[side, z, at:at + 1]

        @pl.when(places[side][0])
        def _():
            halo[side].start()

    for k in range(4):
        @pl.when(jnp.logical_not(places[k][1]))
        def _():
            target = ends[k][1]
            target[...] = jnp.zeros_like(target)

    given = [xf_ref[...], yf_ref[...], zf_ref[...]]
    length = -(-max(a.shape[1] for a in given) // 128) * 128
    lines = []
    for a in given:
        missing = length - a.shape[1]
        lines.append(jnp.concatenate([a, jnp.zeros((1, missing), a.dtype)], 1) if missing else a)
    faces = jnp.concatenate(lines + [jnp.zeros((5, length), jnp.float32)], axis=0)
    nb, bx = xh_ref.shape[0], xh_ref.shape[1]
    nx = nb * bx
    here = WEIGHT * STEP * faces
    above = shifted(here, -1, 0.0)
    e = ladder(here, 1)
    h = ladder(above, -1)
    pivot = above + e
    down = above / pivot
    inverse = 1.0 / pivot
    diag = 1.0 / (e + h - 1.0)
    ups = running_sum(jnp.log(jnp.maximum(here / (here + h), 1e-30)))
    downs = running_sum(jnp.log(jnp.maximum(down, 1e-30)))
    ups_before, downs_before = shifted(ups, 1, 0.0), shifted(downs, 1, 0.0)
    full, next_full = STEP * faces, STEP * shifted(faces, -1, 0.0)
    around = full + next_full

    xp_ref[2:3] = shifted(next_full, 1, 0.0)[0:1, :nx]
    xp_ref[3:4] = next_full[0:1, :nx]
    xp_ref[4:5] = around[0:1, :nx]
    for b in range(nb):
        first, last = b * bx, (b + 1) * bx - 1
        cols = slice(first, last + 1)
        high, low = split(block_of_inverse(diag[0:1, cols], ups[0:1, cols], bx))
        xh_ref[b] = high
        xl_ref[b] = low
        xp_ref[0:1, cols] = jnp.exp(ups[0:1, cols] - ups_before[0:1, first:first + 1])
        xp_ref[1:2, cols] = jnp.exp(downs[0:1, last:last + 1] - downs_before[0:1, cols])

    def own(values, which, start):
        shift = lax.rem(length - start, length)
        return pltpu.roll(values, shift, 1)[which:which + 1]

    def passes(which, start, count):
        u0, d0 = own(ups_before, which, start)[:, 0:1], own(downs_before, which, start)
        u1, d1 = own(ups, which, start), own(downs, which, start)[:, count - 1:count]
        return u1, u0, d1, jnp.exp(jnp.minimum(u1 - u0, 0.0)), jnp.exp(jnp.minimum(d1 - d0, 0.0))

    wide = -(-yc // 128) * 128
    y0 = row * yc
    sums, up_first, down_last, onward, backward = passes(1, y0, yc)
    block = block_of_inverse(own(diag, 1, y0)[:, :wide], sums[:, :wide], wide)[:yc, :yc]
    high = block.astype(jnp.bfloat16).astype(jnp.float32)
    ym_ref[:, 0:yc] = high
    ym_ref[:, yc:2 * yc] = high
    ym_ref[:, 2 * yc:3 * yc] = block - high
    lines = [onward, backward, own(full, 1, y0), own(next_full, 1, y0), own(around, 1, y0)]
    lines = [a[:, :wide] for a in lines] + [jnp.zeros((123, wide), jnp.float32)]
    yt_ref[...] = jnp.transpose(jnp.concatenate(lines, axis=0))[:yc]

    lane = lax.broadcasted_iota(jnp.int32, (1, 128), 1)
    low_weights = high_weights = jnp.zeros((1, 128), jnp.float32)
    for other in range(nr):
        last, first = (other + 1) * yc - 1, other * yc
        value = jnp.exp(jnp.minimum(up_first - ups[1:2, last:last + 1], 0.0))
        low_weights = jnp.where(lane == other, value, low_weights)
        value = jnp.exp(jnp.minimum(downs_before[1:2, first:first + 1] - down_last, 0.0))
        high_weights = jnp.where(lane == other, value, high_weights)

    z0 = col * zc
    _, _, _, onward, backward = passes(2, z0, zc)
    at = lax.broadcasted_iota(jnp.int32, (1, length), 1)
    over = jnp.where(at == zc - 1, own(diag, 2, z0), own(inverse, 2, z0))
    into = jnp.where(at == 0, 0.0, own(here, 2, z0) * over)
    lines = [
        over, into, own(down, 2, z0), own(full, 2, z0), own(next_full, 2, z0), onward, backward,
    ]
    for k, line in enumerate(lines):
        zt_ref[k:k + 1] = line[:, :128]
    zt_ref[7:8] = low_weights
    zt_ref[8:9] = high_weights
    zt_ref[9:10] = own(around, 2, z0)[:, :128]
    zt_ref[10:16] = jnp.zeros((6, 128), jnp.float32)
    for k in range(4):
        @pl.when(places[k][0])
        def _():
            halo[k].wait_send()

        @pl.when(places[k][1])
        def _():
            halo[k].wait_recv()

    fetch.wait()


def on_chip(*shape):
    return pltpu.VMEM(shape, jnp.float32)


def split(a):
    high = a.astype(jnp.bfloat16)
    return high, (a - high.astype(jnp.float32)).astype(jnp.bfloat16)


def dot(a, b):
    return jnp.dot(a, b, preferred_element_type=jnp.float32)


def sweep_kernel(
    planes, zt_ref, u_ref, yhalo_ref, zhalo_ref,
    rea_ref, yt_ref, xh_ref, xl_ref, xp_ref, ym_ref, v_ref, ye_ref, ze_ref,
):
    step, steps = pl.program_id(0), pl.num_programs(0)
    zc, yc, nx = u_ref.shape
    nb, bx = xh_ref.shape[0], xh_ref.shape[1]
    kx, kxn = xp_ref[2:3], xp_ref[3:4]
    ky, kyn = yt_ref[:, 2:3], yt_ref[:, 3:4]
    sub = lax.broadcasted_iota(jnp.int32, (yc, nx), 0)

    @pl.when(step == 0)
    def _():
        v_ref[0] = jnp.zeros((yc, nx), jnp.float32)

    below = jnp.where(step == 0, zhalo_ref[0], u_ref[jnp.maximum(step * planes - 1, 0)])
    above_last = u_ref[jnp.minimum((step + 1) * planes, zc - 1)]
    above_last = jnp.where(step == steps - 1, zhalo_ref[1], above_last)
    changes = []
    for p in range(planes):
        z = step * planes + p
        u = u_ref[z]
        above = u_ref[z + 1] if p + 1 < planes else above_last
        down = jnp.where(sub == 0, yhalo_ref[0, pl.ds(z, 1)], pltpu.roll(u, 1, 0))
        upper = jnp.where(sub == yc - 1, yhalo_ref[1, pl.ds(z, 1)], pltpu.roll(u, yc - 1, 0))
        total = kxn * pltpu.roll(u, nx - 1, 1) + kx * pltpu.roll(u, 1, 1)
        total += kyn * upper + ky * down
        total += zt_ref[4, z] * above + zt_ref[3, z] * below
        centre = STEP * rea_ref[p] * (1.0 - u * u) - (xp_ref[4:5] + (yt_ref[:, 4:5] + zt_ref[9, z]))
        changes.append(total + u * centre)
        below = u
    change = jnp.concatenate(changes, axis=0) if planes > 1 else changes[0]
    local = []
    for b in range(nb):
        high, low = split(change[:, b * bx:(b + 1) * bx])
        local.append(dot(high, xh_ref[b]) + (dot(high, xl_ref[b]) + dot(low, xh_ref[b])))
    rows = planes * yc
    from_left = [jnp.zeros((rows, 1), jnp.float32)]
    from_right = [jnp.zeros((rows, 1), jnp.float32)]
    for b in range(nb - 1):
        through = xp_ref[0:1, (b + 1) * bx - 1:(b + 1) * bx]
        from_left.append(from_left[-1] * through + local[b][:, bx - 1:bx])
        c = nb - 1 - b
        through = xp_ref[1:2, c * bx:c * bx + 1]
        from_right.append(from_right[-1] * through + local[c][:, 0:1])
    from_right.reverse()
    solved = jnp.concatenate(
        [
            local[b]
            + xp_ref[0:1, b * bx:(b + 1) * bx] * from_left[b]
            + xp_ref[1:2, b * bx:(b + 1) * bx] * from_right[b]
            for b in range(nb)
        ],
        axis=1,
    )
    carry = v_ref[jnp.maximum(step * planes - 1, 0)]
    for p in range(planes):
        z = step * planes + p
        high, low = split(solved[p * yc:(p + 1) * yc])
        w = dot(ym_ref[...].astype(jnp.bfloat16), jnp.concatenate([high, low, high], axis=0))
        carry = zt_ref[0, z] * w + zt_ref[1, z] * carry
        v_ref[z] = carry

    @pl.when(step == steps - 1)
    def _():
        wide = 256 if nx % 256 == 0 else nx
        for x in range(nx // wide):
            cols = slice(x * wide, (x + 1) * wide)
            top = v_ref[zc - 1, :, cols]
            ze_ref[1, :, cols] = top
            ye_ref[0, zc - 1:zc, cols] = top[0:1]
            ye_ref[1, zc - 1:zc, cols] = top[yc - 1:yc]

            def back(i, value):
                z = zc - 2 - i
                value = v_ref[z, :, cols] + zt_ref[2, z] * value
                v_ref[z, :, cols] = value
                ye_ref[0, pl.ds(z, 1), cols] = value[0:1]
                ye_ref[1, pl.ds(z, 1), cols] = value[yc - 1:yc]
                return value

            ze_ref[0, :, cols] = lax.fori_loop(0, zc - 1, back, top)


def exchange_kernel(
    nr, nc, chunks, zt_ref, yp_ref, ye_ref, ze_ref, sy_ref, sz_ref,
    ybuf, zbuf, zsend, esend, ebuf, ysend_sem, yrecv_sem, zsend_sem, zrecv_sem,
    esend_sem, erecv_sem,
):
    row, col = lax.axis_index("row"), lax.axis_index("col")
    zc, nx = ye_ref.shape[1], ye_ref.shape[2]
    yc = ze_ref.shape[1]
    has_low, has_high = col > 0, col < nc - 1
    barrier = pltpu.get_barrier_semaphore()
    for other in range(nr):
        @pl.when(other != row)
        def _():
            pl.semaphore_signal(barrier, inc=1, device_id=(other, col), device_id_type=MESH)

    @pl.when(has_low)
    def _():
        pl.semaphore_signal(barrier, inc=1, device_id=(row, col - 1), device_id_type=MESH)

    @pl.when(has_high)
    def _():
        pl.semaphore_signal(barrier, inc=1, device_id=(row, col + 1), device_id_type=MESH)

    pl.semaphore_wait(barrier, nr - 1 + has_low.astype(jnp.int32) + has_high.astype(jnp.int32))

    def y_copy(side, other, slot):
        return pltpu.make_async_remote_copy(
            src_ref=ye_ref.at[1 - side],
            dst_ref=ybuf.at[side, slot],
            send_sem=ysend_sem.at[side, other],
            recv_sem=yrecv_sem.at[side, slot],
            device_id=(other, col),
            device_id_type=MESH,
        )

    for other in range(nr):
        @pl.when(other > row)
        def _():
            y_copy(0, other, row).start()

        @pl.when(other < row)
        def _():
            y_copy(1, other, row).start()

    part = yc // chunks

    def z_copy(side, k):
        rows = pl.ds(k * part, part)
        return pltpu.make_async_remote_copy(
            src_ref=zsend.at[side, rows],
            dst_ref=zbuf.at[side, rows],
            send_sem=zsend_sem.at[side, k],
            recv_sem=zrecv_sem.at[side, k],
            device_id=(row, col + (1 - 2 * side)),
            device_id_type=MESH,
        )

    def scan(side):
        source, target = (has_low, has_high) if side == 0 else (has_high, has_low)
        edge, z = (1, zc - 1) if side == 0 else (0, 0)
        through = zt_ref[5 + side, z]
        for k in range(chunks):
            rows = slice(k * part, (k + 1) * part)

            @pl.when(source)
            def _():
                z_copy(side, k).wait_recv()
                sz_ref[side, rows] = zbuf[side, rows]

            @pl.when(jnp.logical_not(source))
            def _():
                sz_ref[side, rows] = jnp.zeros((part, nx), jnp.float32)

            @pl.when(target)
            def _():
                zsend[side, rows] = ze_ref[edge, rows] + through * sz_ref[side, rows]
                z_copy(side, k).start()

    low_half = col < nc // 2

    @pl.when(low_half)
    def _():
        scan(0)

    scan(1)

    @pl.when(jnp.logical_not(low_half))
    def _():
        scan(0)

    for k in range(2):
        esend[0, k:k + 1] = sz_ref[k, yc - 1:yc]
        esend[1, k:k + 1] = sz_ref[k, 0:1]

    def e_copy(side, other, slot):
        return pltpu.make_async_remote_copy(
            src_ref=esend.at[side],
            dst_ref=ebuf.at[side, slot],
            send_sem=esend_sem.at[side, other],
            recv_sem=erecv_sem.at[side, slot],
            device_id=(other, col),
            device_id_type=MESH,
        )

    for other in range(nr):
        @pl.when(other > row)
        def _():
            e_copy(0, other, row).start()

        @pl.when(other < row)
        def _():
            e_copy(1, other, row).start()

    sy_ref[...] = jnp.zeros_like(sy_ref)
    for other in range(nr):
        @pl.when(other < row)
        def _():
            y_copy(0, other, other).wait_recv()
            sy_ref[0] += zt_ref[7, other] * ybuf[0, other]

        @pl.when(other > row)
        def _():
            y_copy(1, other, other).wait_recv()
            sy_ref[1] += zt_ref[8, other] * ybuf[1, other]

    for other in range(nr):
        for side, here in ((0, other < row), (1, other > row)):
            @pl.when(here)
            def _():
                e_copy(side, other, other).wait_recv()
                coefficients = zt_ref[7 + side, other] * yp_ref[:, side:side + 1]
                for k in range(2):
                    sz_ref[k] += coefficients * ebuf[side, other, k:k + 1]

    for k in range(chunks):
        @pl.when(has_high)
        def _():
            z_copy(0, k).wait_send()

        @pl.when(has_low)
        def _():
            z_copy(1, k).wait_send()

    for other in range(nr):
        for side, there in ((0, other > row), (1, other < row)):
            @pl.when(there)
            def _():
                y_copy(side, other, row).wait_send()
                e_copy(side, other, row).wait_send()


def finish_kernel(planes, zt_ref, u_ref, v_ref, yp_ref, sy_ref, sz_ref, out_ref):
    yb, ya = yp_ref[:, 0:1], yp_ref[:, 1:2]
    for p in range(planes):
        z = pl.program_id(0) * planes + p
        value = u_ref[z] + v_ref[z]
        value += yb * sy_ref[0, pl.ds(z, 1)] + ya * sy_ref[1, pl.ds(z, 1)]
        out_ref[p] = value + zt_ref[5, z] * sz_ref[0] + zt_ref[6, z] * sz_ref[1]


def body(u, reaction, x_faces, y_faces, z_faces, x_inverse, y_inverse, z_inverse):
    zc, yc, nx = u.shape
    nr, nc = lax.axis_size("row"), lax.axis_size("col")
    f32 = jnp.float32

    tall = 8 if yc % 8 == 0 else yc
    bx = 256 if nx % 256 == 0 else nx
    nb = nx // bx
    smem = pl.BlockSpec(memory_space=pltpu.SMEM)
    vmem = pl.BlockSpec(memory_space=pltpu.VMEM)
    xh, xl, xp, ym, yt, zt, held, yhalo, zhalo = pl.pallas_call(
        functools.partial(table_kernel, nr, nc),
        in_specs=[vmem, vmem, vmem, pl.BlockSpec(memory_space=pltpu.HBM)],
        out_specs=[vmem] * 9,
        out_shape=[
            jax.ShapeDtypeStruct((nb, bx, bx), jnp.bfloat16),
            jax.ShapeDtypeStruct((nb, bx, bx), jnp.bfloat16),
            jax.ShapeDtypeStruct((8, nx), f32),
            jax.ShapeDtypeStruct((yc, 3 * yc), f32),
            jax.ShapeDtypeStruct((yc, 128), f32),
            jax.ShapeDtypeStruct((16, 128), f32),
            on_chip(zc, yc, nx),
            on_chip(2, zc, nx),
            on_chip(2, yc, nx),
        ],
        scratch_shapes=[
            pltpu.VMEM((2, zc, tall, nx), f32),
            pltpu.VMEM((2, zc, nx), f32),
            pltpu.SemaphoreType.DMA(()),
            pltpu.SemaphoreType.DMA((2,)),
            pltpu.SemaphoreType.DMA((4,)),
            pltpu.SemaphoreType.DMA((4,)),
        ],
        compiler_params=pltpu.CompilerParams(
            collective_id=1, has_side_effects=True, vmem_limit_bytes=VMEM_LIMIT
        ),
        cost_estimate=pl.CostEstimate(flops=40000000, bytes_accessed=1 << 20, transcendentals=0),
    )(x_faces[None], y_faces[None], z_faces[None], pltpu.with_memory_space_constraint(u, pltpu.HBM))

    planes = next(p for p in (8, 4, 2, 1) if zc % p == 0)
    last = next(p for p in (8, 4, 2, 1) if zc % p == 0)
    reaction = pltpu.with_memory_space_constraint(reaction, pltpu.HBM)

    slab = pl.BlockSpec((planes, yc, nx), lambda step: (step, 0, 0))
    v, ye, ze = pl.pallas_call(
        functools.partial(sweep_kernel, planes),
        grid=(zc // planes,),
        in_specs=[
            smem, vmem, vmem, vmem, slab,
            vmem, vmem, vmem, vmem, vmem,
        ],
        out_specs=[vmem, vmem, vmem],
        out_shape=[
            on_chip(zc, yc, nx),
            jax.ShapeDtypeStruct((2, zc, nx), f32),
            jax.ShapeDtypeStruct((2, yc, nx), f32),
        ],
        compiler_params=pltpu.CompilerParams(vmem_limit_bytes=VMEM_LIMIT),
    )(zt, held, yhalo, zhalo, reaction, yt, xh, xl, xp, ym)

    chunks = yc // 8 if yc % 8 == 0 else 1
    sy, sz = pl.pallas_call(
        functools.partial(exchange_kernel, nr, nc, chunks),
        in_specs=[smem, vmem, vmem, vmem],
        out_specs=[vmem, vmem],
        out_shape=[
            jax.ShapeDtypeStruct((2, zc, nx), f32),
            jax.ShapeDtypeStruct((2, yc, nx), f32),
        ],
        scratch_shapes=[
            pltpu.VMEM((2, nr, zc, nx), f32),
            pltpu.VMEM((2, yc, nx), f32),
            pltpu.VMEM((2, yc, nx), f32),
            pltpu.VMEM((2, 2, nx), f32),
            pltpu.VMEM((2, nr, 2, nx), f32),
            pltpu.SemaphoreType.DMA((2, nr)),
            pltpu.SemaphoreType.DMA((2, nr)),
            pltpu.SemaphoreType.DMA((2, chunks)),
            pltpu.SemaphoreType.DMA((2, chunks)),
            pltpu.SemaphoreType.DMA((2, nr)),
            pltpu.SemaphoreType.DMA((2, nr)),
        ],
        compiler_params=pltpu.CompilerParams(
            collective_id=0, has_side_effects=True, vmem_limit_bytes=VMEM_LIMIT
        ),
    )(zt, yt, ye, ze)

    return pl.pallas_call(
        functools.partial(finish_kernel, last),
        grid=(zc // last,),
        in_specs=[smem, vmem, vmem, vmem, vmem, vmem],
        out_specs=pl.BlockSpec((last, yc, nx), lambda step: (step, 0, 0)),
        out_shape=jax.ShapeDtypeStruct((zc, yc, nx), f32),
        compiler_params=pltpu.CompilerParams(vmem_limit_bytes=VMEM_LIMIT),
    )(zt, held, v, yt, sy, sz)


def solution(mesh):
    in_specs = (P("col", "row", None), P("col", "row", None), P(), P(), P(), P(), P(), P())
    out_specs = P("col", "row", None)
    return jax.shard_map(body, mesh=mesh, in_specs=in_specs, out_specs=out_specs, check_vma=False)
```

profile of v0, /device:TPU:0, one launch (start us, length us, event | category | flops | bytes accessed | tf_op | source)
XLA Modules:
  0.0 61.5 jit_solution(11054574599516732450)
XLA Ops:
  0.0 0.0 copy-start
  0.0 0.7 %copy-done = f32[1024]{0:T(1024)S(1)} copy-done((f32[1024]{0:T(1024)S(1)}, f32[1024]{0:T(1024)}, u32[]{:S(2)}) %copy-start) | copy-done | bytes 4120
  0.7 0.0 copy-start.1
  0.7 0.7 %copy-done.1 = f32[256]{0:T(256)S(1)} copy-done((f32[256]{0:T(256)S(1)}, f32[256]{0:T(256)}, u32[]{:S(2)}) %copy-start.1) | copy-done | bytes 1048
  1.4 0.0 copy-start.2
  1.4 0.7 %copy-done.2 = f32[256]{0:T(256)S(1)} copy-done((f32[256]{0:T(256)S(1)}, f32[256]{0:T(256)}, u32[]{:S(2)}) %copy-start.2) | copy-done | bytes 1048
  2.0 11.3 %shard_map.55 = (bf16[4,256,256]{2,1,0:T(8,128)(2,1)S(1)}, bf16[4,256,256]{2,1,0:T(8,128)(2,1)S(1)}, f32[8,1024]{1,0:T(8,128)S(1)}, f32[64,192]{1,0:T(8,128)S(1)...) custom-call(f32[1,1024]{1,0:T(1,128)S(1)} %bitcast.3, ...), custom_call_target="tpu_custom_call" | custom-call | flops 40000000 | bytes 1048576 | tf_op jit(solution)/shard_map/pallas_call | solution.py:483
  13.3 20.5 %shard_map.56 = (f32[32,64,1024]{2,1,0:T(8,128)S(1)}, f32[2,32,1024]{2,1,0:T(8,128)S(1)}, f32[2,64,1024]{2,1,0:T(8,128)S(1)}) custom-call(f32[16,128]{1,0:T(8,128)S(1)} %get-tuple-element.19.zt_ref, f32[32,64,1024]{2,1,0:T(8,128)S(1)} %get-tuple-element.20.u_ref, f32[2,32,1024]{2,1,0:T(8,128)S(1)} %get-tuple-element.21.yhalo_ref, ...), custom_call_target="tpu_custom_call" | custom-call | tf_op jit(solution)/shard_map/pallas_call | solution.py:517
  33.8 20.6 %shard_map.57 = (f32[2,32,1024]{2,1,0:T(8,128)S(1)}, f32[2,64,1024]{2,1,0:T(8,128)S(1)}) custom-call(f32[16,128]{1,0:T(8,128)S(1)} %get-tuple-element.19.zt_ref, f32[64,128]{1,0:T(8,128)S(1)} %get-tuple-element.23.yt_ref.yp_ref, f32[2,32,1024]{2,1,0:T(8,128)S(1)} %get-tuple-element.29.ye_ref, f32[2,64,1024]{2,1,0:T(8,128)S(1)} %get-tuple-element.30.ze_ref), custom_call_target="tpu_custom_call" | custom-call | tf_op jit(solution)/shard_map/pallas_call | solution.py:534
  54.4 7.1 %shard_map.58 = f32[32,64,1024]{2,1,0:T(8,128)} custom-call(f32[16,128]{1,0:T(8,128)S(1)} %get-tuple-element.19.zt_ref, f32[32,64,1024]{2,1,0:T(8,128)S(1)} %get-tuple-element.20.u_ref, f32[32,64,1024]{2,1,0:T(8,128)S(1)} %get-tuple-element.28.v_ref, f32[64,128]{1,0:T(8,128)S(1)} %get-tuple-element.23.yt_ref.yp_ref, ...), custom_call_target="tpu_custom_call" | custom-call | tf_op jit(solution)/shard_map/pallas_call | solution.py:560
Async XLA Ops:
  0.0 0.7 %copy-start = (f32[1024]{0:T(1024)S(1)}, f32[1024]{0:T(1024)}, u32[]{:S(2)}) copy-start(f32[1024]{0:T(1024)} %param.10) | copy-start | bytes 12292
  0.7 0.7 %copy-start.1 = (f32[256]{0:T(256)S(1)}, f32[256]{0:T(256)}, u32[]{:S(2)}) copy-start(f32[256]{0:T(256)} %param.11) | copy-start | bytes 3076
  1.4 0.7 %copy-start.2 = (f32[256]{0:T(256)S(1)}, f32[256]{0:T(256)}, u32[]{:S(2)}) copy-start(f32[256]{0:T(256)} %param.12) | copy-start | bytes 3076
where the time goes:
time: 61.8 us; the launch traced here: 61.5 us
  Pallas kernels  59.5 us (96%)
  local copies, waits for them, and re-layouts  2.04 us (3%)
    pallas_call x1, Pallas kernels, body(): pl.pallas_call(functools.partial(exchange_kernel, nr, nc, chunks), in_spe...  20.6 us
    pallas_call x1, Pallas kernels, body(): pl.pallas_call(functools.partial(sweep_kernel, planes), grid=(zc // plane...  20.5 us
    pallas_call x1, Pallas kernels, body(): pl.pallas_call(functools.partial(table_kernel, nr, nc), in_specs=[vmem, v...  11.3 us
    pallas_call x1, Pallas kernels, body(): pl.pallas_call(functools.partial(finish_kernel, last), grid=(zc // last,)...  7.12 us
    unnamed x6, local copies, waits for them, and re-layouts  2.04 us

commit v1 on v0

v1 whole, which is shorter than its diff:
```python
import functools

import jax
import jax.numpy as jnp
from jax import lax
from jax.experimental import pallas as pl
from jax.experimental.pallas import tpu as pltpu
from jax.sharding import PartitionSpec as P

WEIGHT = 0.5
STEP = 1000.0
MESH = pl.DeviceIdType.MESH
LANES = 128
MAIN_VMEM = 24 * 1024 * 1024
LAST_VMEM = 12 * 1024 * 1024


def shifted(a, by, fill):
    n = a.shape[1]
    lane = lax.broadcasted_iota(jnp.int32, a.shape, 1)
    if by > 0:
        return jnp.where(lane >= by, pltpu.roll(a, by, 1), fill)
    return jnp.where(lane < n + by, pltpu.roll(a, n + by, 1), fill)


def running_sum(a):
    by = 1
    while by < a.shape[1]:
        a = a + shifted(a, by, 0.0)
        by *= 2
    return a


def ladder(couple, sign):
    p00, p01, p10, p11 = 1.0 + couple, couple, jnp.ones_like(couple), couple
    by = 1
    while by < couple.shape[1]:
        q00, q01 = shifted(p00, sign * by, 1.0), shifted(p01, sign * by, 0.0)
        q10, q11 = shifted(p10, sign * by, 0.0), shifted(p11, sign * by, 1.0)
        n00, n01 = p00 * q00 + p01 * q10, p00 * q01 + p01 * q11
        n10, n11 = p10 * q00 + p11 * q10, p10 * q01 + p11 * q11
        scale = 1.0 / (n00 + n01 + n10 + n11)
        p00, p01, p10, p11 = n00 * scale, n01 * scale, n10 * scale, n11 * scale
        by *= 2
    return p00 / p10


def as_column(line, rows):
    n = line.shape[1]
    return jnp.transpose(jnp.broadcast_to(line, (n, n)))[:rows, :rows]


def block_of_inverse(diagonal, sums, n):
    i = lax.broadcasted_iota(jnp.int32, (n, n), 0)
    j = lax.broadcasted_iota(jnp.int32, (n, n), 1)
    near = jnp.where(i >= j, diagonal[:, :n], as_column(diagonal, n))
    return near * jnp.exp(-jnp.abs(as_column(sums, n) - sums[:, :n]))


def split(a):
    high = a.astype(jnp.bfloat16)
    return high, (a - high.astype(jnp.float32)).astype(jnp.bfloat16)


def dot(a, b):
    return jnp.dot(a, b, preferred_element_type=jnp.float32)


def lanes_of(column):
    return jnp.broadcast_to(column, (column.shape[0], LANES))


def x_solve(rows_of, xw, xpass, xthrough, nt):
    nb, bx = xw.shape[0], xw.shape[2]
    per = bx // LANES
    local = []
    for b in range(nb):
        high, low = split(jnp.concatenate([rows_of(b * per + i) for i in range(per)], axis=1))
        local.append(dot(jnp.concatenate([high, low, high], axis=1), xw[b]))
    left, right = [None], [None]
    for b in range(nb - 1):
        value = lanes_of(local[b][:, bx - 1:bx])
        if b:
            value = value + left[-1] * xthrough[0, b:b + 1]
        left.append(value)
        c = nb - 1 - b
        value = lanes_of(local[c][:, 0:1])
        if b:
            value = value + right[-1] * xthrough[1, c:c + 1]
        right.append(value)
    right.reverse()
    solved = []
    for t in range(nt):
        b, i = t // per, t % per
        value = local[b][:, i * LANES:(i + 1) * LANES]
        if b:
            value = value + xpass[0, t:t + 1] * left[b]
        if b < nb - 1:
            value = value + xpass[1, t:t + 1] * right[b]
        solved.append(value)
    return solved


def main_kernel(
    nr, nc, planes, xf_hbm, yf_hbm, zf_hbm, field_ref, rea_ref,
    base, sy_ref, sz_ref, zpass, ypass,
    faces, u, edges, yhalo, coef, xface, yface, ztab, xline, xw, xpass, xthrough, ym, weights,
    vprev, zedge, zsend, zbuf, ye, ybuf, esend, ebuf, fill,
    face_sem, u_sem, rea_sem, hsend, hrecv, zsend_sem, zrecv_sem,
    ysend_sem, yrecv_sem, esend_sem, erecv_sem,
):
    row, col = lax.axis_index("row"), lax.axis_index("col")
    nt, zc, yc, _ = base.shape
    nx = nt * LANES
    nk = yc // 8
    length = faces.shape[2]
    f32 = jnp.float32

    face_copies = [
        pltpu.make_async_copy(
            a, faces.at[i, pl.ds(0, 1), pl.ds(0, a.shape[1])], face_sem.at[i]
        )
        for i, a in enumerate((xf_hbm, yf_hbm, zf_hbm))
    ]
    for i, a in enumerate((xf_hbm, yf_hbm, zf_hbm)):
        if a.shape[1] < length:
            faces[i, 0:1, a.shape[1]:] = jnp.zeros((1, length - a.shape[1]), f32)
    for copy in face_copies:
        copy.start()
    u_copies = [
        pltpu.make_async_copy(
            field_ref.at[:, :, pl.ds(t * LANES, LANES)], u.at[t, :, pl.ds(8, yc)], u_sem.at[t]
        )
        for t in range(nt)
    ]
    for copy in u_copies:
        copy.start()

    up_row, down_row = row < nr - 1, row > 0
    has_low, has_high = col > 0, col < nc - 1
    barrier = pltpu.get_barrier_semaphore()
    for other in range(nr):
        @pl.when(other != row)
        def _():
            pl.semaphore_signal(barrier, inc=1, device_id=(other, col), device_id_type=MESH)

    @pl.when(has_low)
    def _():
        pl.semaphore_signal(barrier, inc=1, device_id=(row, col - 1), device_id_type=MESH)

    @pl.when(has_high)
    def _():
        pl.semaphore_signal(barrier, inc=1, device_id=(row, col + 1), device_id_type=MESH)

    vprev[...] = jnp.zeros_like(vprev)
    for side, source, there in ((0, has_low, down_row), (1, has_high, up_row)):
        @pl.when(jnp.logical_not(source))
        def _():
            zbuf[side] = jnp.zeros(zbuf.shape[1:], f32)

        @pl.when(jnp.logical_not(there))
        def _():
            yhalo[side] = jnp.zeros(yhalo.shape[1:], f32)

    for copy in face_copies:
        copy.wait()

    lines = jnp.concatenate([faces[0, 0:1], faces[1, 0:1], faces[2, 0:1], jnp.zeros((5, length), f32)], axis=0)
    here = WEIGHT * STEP * lines
    above = shifted(here, -1, 0.0)
    e = ladder(here, 1)
    h = ladder(above, -1)
    pivot = above + e
    down = above / pivot
    inverse = 1.0 / pivot
    diag = 1.0 / (e + h - 1.0)
    ups = running_sum(jnp.log(jnp.maximum(here / (here + h), 1e-30)))
    downs = running_sum(jnp.log(jnp.maximum(down, 1e-30)))
    ups_before, downs_before = shifted(ups, 1, 0.0), shifted(downs, 1, 0.0)
    next_lines = shifted(lines, -1, 0.0)
    around = lines + next_lines

    xline[0:1] = diag[0:1, :nx]
    xline[1:2] = ups[0:1, :nx]
    xline[2:3] = ups_before[0:1, :nx]
    xline[3:4] = downs[0:1, :nx]
    xline[4:5] = downs_before[0:1, :nx]
    before = shifted(next_lines, 1, 0.0)
    for t in range(nt):
        cols = slice(t * LANES, (t + 1) * LANES)
        xface[0, t:t + 1] = before[0:1, cols]
        xface[1, t:t + 1] = next_lines[0:1, cols]

    def own(values, which, start):
        shift = lax.rem(length - start, length)
        return pltpu.roll(values, shift, 1)[which:which + 1]

    def passes(which, start, count):
        u0, d0 = own(ups_before, which, start)[:, 0:1], own(downs_before, which, start)
        u1, d1 = own(ups, which, start), own(downs, which, start)[:, count - 1:count]
        return u1, u0, d1, jnp.exp(jnp.minimum(u1 - u0, 0.0)), jnp.exp(jnp.minimum(d1 - d0, 0.0))

    def columns(given):
        filled = [a[:, :LANES] for a in given] + [jnp.zeros((LANES - len(given), LANES), f32)]
        return jnp.transpose(jnp.concatenate(filled, axis=0))

    z0 = col * zc
    zsums, _, _, onward, backward = passes(2, z0, zc)
    at = lax.broadcasted_iota(jnp.int32, (1, length), 1)
    zdiag = own(diag, 2, z0)
    over = jnp.where(at == zc - 1, zdiag, own(inverse, 2, z0))
    into = jnp.where(at == 0, 0.0, own(here, 2, z0) * over)
    low_end = zdiag[:, 0:1] * jnp.exp(jnp.minimum(zsums - zsums[:, 0:1], 0.0))
    scale = WEIGHT * STEP
    turned = columns([scale * over, into, scale * low_end, own(down, 2, z0), onward, backward])
    for i in range(4):
        ztab[i] = lanes_of(turned[:zc, i:i + 1])
    for i in range(2):
        zpass[i] = lanes_of(turned[:zc, 4 + i:5 + i])

    y0 = row * yc
    sums, up_first, down_last, onward, backward = passes(1, y0, yc)
    ky, kyn, kya = own(lines, 1, y0), own(next_lines, 1, y0), own(around, 1, y0)
    turned = columns([ky, kyn, 1.0 / scale - kya, onward, backward])
    yface[0] = lanes_of(turned[:yc, 0:1])
    yface[1] = lanes_of(turned[:yc, 1:2])
    ypass[0] = lanes_of(turned[:yc, 3:4])
    ypass[1] = lanes_of(turned[:yc, 4:5])
    ycoef = lanes_of(turned[:yc, 2:3])
    for t in range(nt):
        coef[t] = ycoef - around[0:1, t * LANES:(t + 1) * LANES]
    block = block_of_inverse(own(diag, 1, y0)[:, :LANES], sums[:, :LANES], LANES)[:yc, :yc]
    high, low = split(block)
    ym[...] = jnp.concatenate([high, high, low], axis=1)
    for other in range(nr):
        last, first = (other + 1) * yc - 1, other * yc
        value = jnp.exp(jnp.minimum(up_first - ups[1:2, last:last + 1], 0.0))
        weights[0, other:other + 1] = lanes_of(value)
        value = jnp.exp(jnp.minimum(downs_before[1:2, first:first + 1] - down_last, 0.0))
        weights[1, other:other + 1] = lanes_of(value)

    def rea_copy(k, t):
        rows = pl.ds(pl.multiple_of(k * 8, 8), 8)
        return pltpu.make_async_copy(
            rea_ref.at[:, rows, pl.ds(t * LANES, LANES)], base.at[t, :, rows], rea_sem.at[k, t]
        )

    def start_rea(i, _):
        k = lax.rem(i + 1, nk)
        for t in range(nt):
            rea_copy(k, t).start()
        return 0

    lax.fori_loop(0, nk, start_rea, 0)
    for copy in u_copies:
        copy.wait()

    def take_edges(z, _):
        for t in range(nt):
            edges[0, t, pl.ds(z, 1)] = u[t, z, 8 + yc - 1:8 + yc]
            edges[1, t, pl.ds(z, 1)] = u[t, z, 8:9]
        return 0

    lax.fori_loop(0, zc, take_edges, 0, unroll=4 if zc % 4 == 0 else 1)
    pl.semaphore_wait(barrier, nr - 1 + has_low.astype(jnp.int32) + has_high.astype(jnp.int32))

    def halo(side):
        return pltpu.make_async_remote_copy(
            src_ref=edges.at[side], dst_ref=yhalo.at[side],
            send_sem=hsend.at[side], recv_sem=hrecv.at[side],
            device_id=(row + 1 - 2 * side, col), device_id_type=MESH,
        )

    for side, to in ((0, up_row), (1, down_row)):
        @pl.when(to)
        def _():
            halo(side).start()

    def z_copy(side, k):
        return pltpu.make_async_remote_copy(
            src_ref=zsend.at[side, k], dst_ref=zbuf.at[side, k],
            send_sem=zsend_sem.at[side, k], recv_sem=zrecv_sem.at[side, k],
            device_id=(row, col + (1 - 2 * side)), device_id_type=MESH,
        )

    far = (col, nc - 1 - col)

    def relay(side, k):
        source, target = (has_low, has_high) if side == 0 else (has_high, has_low)
        at_row = zc - 1 if side == 0 else 0

        @pl.when(source)
        def _():
            z_copy(side, k).wait_recv()

        @pl.when(target)
        def _():
            through = zpass[side, at_row:at_row + 1]
            for t in range(nt):
                zsend[side, k, t] = zedge[side, k, t] + through * zbuf[side, k, t]
            z_copy(side, k).start()

    lane = lax.broadcasted_iota(jnp.int32, (8, LANES), 1)
    group = min(nt, 8)

    def first_pass(i, _):
        k = lax.rem(i + 1, nk)
        y = pl.multiple_of(k * 8, 8)
        rows = pl.ds(y, 8)
        for t in range(nt):
            rea_copy(k, t).wait()

        @pl.when(i == nk - 2)
        def _():
            for side, there in ((0, down_row), (1, up_row)):
                @pl.when(there)
                def _():
                    halo(side).wait_recv()

            def put(z, _):
                for t in range(nt):
                    u[t, z, 7:8] = yhalo[0, t, pl.ds(z, 1)]
                    u[t, z, 8 + yc:9 + yc] = yhalo[1, t, pl.ds(z, 1)]
                return 0

            lax.fori_loop(0, zc, put, 0, unroll=4 if zc % 4 == 0 else 1)

        for g in range(nt // group):
            tiles = [g * group + i for i in range(group)]

            def one(z, carried):
                tops, lows = carried
                over, into, low_end = ztab[0, pl.ds(z, 1)], ztab[1, pl.ds(z, 1)], ztab[2, pl.ds(z, 1)]
                kyd, kyu = yface[0, rows], yface[1, rows]
                middle = [u[t % nt, z, pl.ds(y + 8, 8)] for t in range(tiles[0] - 1, tiles[-1] + 2)] \
                    if group < nt else [u[t, z, pl.ds(y + 8, 8)] for t in tiles]
                from_low = [pltpu.roll(a, 1, 1) for a in middle]
                from_high = [pltpu.roll(a, LANES - 1, 1) for a in middle]
                n, shift = len(middle), 1 if group < nt else 0
                new_tops, new_lows = [], []
                for j, t in enumerate(tiles):
                    m = j + shift
                    c = middle[m]
                    left = jnp.where(lane == 0, from_low[(m - 1) % n], from_low[m])
                    right = jnp.where(lane == LANES - 1, from_high[(m + 1) % n], from_high[m])
                    q = base[t, z, rows] * (1.0 - c * c) + coef[t, rows]
                    value = q * c + (xface[1, t:t + 1] * right + xface[0, t:t + 1] * left)
                    value = value + (kyu * u[t, z, pl.ds(y + 9, 8)] + kyd * u[t, z, pl.ds(y + 7, 8)])
                    top = over * value + into * tops[j]
                    base[t, z, rows] = top
                    new_tops.append(top)
                    new_lows.append(lows[j] + low_end * value)
                return new_tops, new_lows

            zero = [jnp.zeros((8, LANES), f32) for _ in tiles]
            tops, lows = lax.fori_loop(0, zc, one, (zero, zero), unroll=2 if zc % 2 == 0 else 1)
            for j, t in enumerate(tiles):
                zedge[0, k, t] = tops[j]
                zedge[1, k, t] = lows[j]

        for side in (0, 1):
            turn = i - 2 * far[side]

            @pl.when(turn >= 0)
            def _():
                relay(side, lax.rem(turn + 1, nk))

        return 0

    lax.fori_loop(0, nk, first_pass, 0)

    def slot_of(d):
        return 5 * ((d + 1) // 2) + 9 * (d // 2)

    def relays(slot):
        for side in (0, 1):
            d = far[side]
            turn = slot - (slot_of(d) - (nk - 1))

            @pl.when((turn >= jnp.maximum(nk - 2 * d, 0)) & (turn < nk))
            def _():
                relay(side, lax.rem(turn + 1, nk))

    per = 256 // LANES
    steps = zc // planes

    def y_solve(tiles):
        high, low = split(jnp.concatenate(tiles, axis=1))
        return dot(ym[...], jnp.concatenate([high, low, high], axis=0))

    def second_pass(slot, _):
        for p in range(planes):
            z = zc - 1 - (slot * planes + p)
            falling = ztab[3, pl.ds(z, 1)]
            for b in range(nt // per):
                ready = []
                for t in range(b * per, (b + 1) * per):
                    v = base[t, z] + falling * vprev[t]
                    vprev[t] = v
                    ready.append(v - u[t, z, 8:8 + yc])
                solved = y_solve(ready)
                for i in range(per):
                    t = b * per + i
                    part = solved[:, i * LANES:(i + 1) * LANES]
                    base[t, z] = part
                    ye[0, t, pl.ds(z, 1)] = part[0:1]
                    ye[1, t, pl.ds(z, 1)] = part[yc - 1:yc]
        relays(slot)
        return 0

    lax.fori_loop(0, steps, second_pass, 0)

    def y_copy(side, other, slot):
        return pltpu.make_async_remote_copy(
            src_ref=ye.at[1 - side], dst_ref=ybuf.at[side, slot],
            send_sem=ysend_sem.at[side, other], recv_sem=yrecv_sem.at[side, slot],
            device_id=(other, col), device_id_type=MESH,
        )

    for other in range(nr):
        @pl.when(other > row)
        def _():
            y_copy(0, other, row).start()

        @pl.when(other < row)
        def _():
            y_copy(1, other, row).start()

    nb, bx = xw.shape[0], xw.shape[2]
    for b in range(nb):
        cols = slice(b * bx, (b + 1) * bx)
        first, last = b * bx, (b + 1) * bx - 1
        high, low = split(block_of_inverse(xline[0:1, cols], xline[1:2, cols], bx) * (1.0 / WEIGHT))
        xw[b, 0:bx] = high
        xw[b, bx:2 * bx] = high
        xw[b, 2 * bx:3 * bx] = low
        ahead = jnp.exp(xline[1:2, cols] - xline[2:3, first:first + 1])
        back = jnp.exp(xline[3:4, last:last + 1] - xline[4:5, cols])
        for i in range(bx // LANES):
            t = b * (bx // LANES) + i
            xpass[0, t:t + 1] = ahead[:, i * LANES:(i + 1) * LANES]
            xpass[1, t:t + 1] = back[:, i * LANES:(i + 1) * LANES]
        xthrough[0, b:b + 1] = lanes_of(ahead[:, bx - 1:bx])
        xthrough[1, b:b + 1] = lanes_of(back[:, 0:1])

    def third_pass(slot, _):
        zs = [slot * planes + p for p in range(planes)]
        solved = x_solve(
            lambda t: jnp.concatenate([base[t, z] for z in zs], axis=0), xw, xpass, xthrough, nt
        )
        for t in range(nt):
            for p, z in enumerate(zs):
                base[t, z] = u[t, z, 8:8 + yc] + solved[t][p * yc:(p + 1) * yc]
        relays(steps + slot)
        return 0

    lax.fori_loop(0, steps, third_pass, 0)

    def tail(slot, _):
        relays(slot)
        return 0

    most = slot_of(nc - 1) + 1
    lax.fori_loop(2 * steps, max(2 * steps, most), tail, 0)

    for k in range(2):
        for b in range(nt // per):
            tiles = [
                jnp.concatenate([zbuf[k, j, t] for j in range(nk)], axis=0)
                for t in range(b * per, (b + 1) * per)
            ]
            solved = y_solve(tiles)
            for i in range(per):
                t = b * per + i
                part = solved[:, i * LANES:(i + 1) * LANES]
                fill[k, t] = part
                esend[0, t, k:k + 1] = part[yc - 1:yc]
                esend[1, t, k:k + 1] = part[0:1]

    def e_copy(side, other, slot):
        return pltpu.make_async_remote_copy(
            src_ref=esend.at[side], dst_ref=ebuf.at[side, slot],
            send_sem=esend_sem.at[side, other], recv_sem=erecv_sem.at[side, slot],
            device_id=(other, col), device_id_type=MESH,
        )

    for other in range(nr):
        @pl.when(other > row)
        def _():
            e_copy(0, other, row).start()

        @pl.when(other < row)
        def _():
            e_copy(1, other, row).start()

    sy_ref[...] = jnp.zeros_like(sy_ref)
    for other in range(nr):
        for side, there in ((0, other < row), (1, other > row)):
            @pl.when(there)
            def _():
                y_copy(side, other, other).wait_recv()
                for t in range(nt):
                    sy_ref[side, t] += weights[side, other:other + 1] * ybuf[side, other, t]

    solved = x_solve(
        lambda t: jnp.concatenate([sy_ref[0, t], sy_ref[1, t]], axis=0), xw, xpass, xthrough, nt
    )
    for t in range(nt):
        sy_ref[0, t] = solved[t][:zc]
        sy_ref[1, t] = solved[t][zc:]

    for other in range(nr):
        for side, there in ((0, other < row), (1, other > row)):
            @pl.when(there)
            def _():
                e_copy(side, other, other).wait_recv()
                coefficients = weights[side, other:other + 1] * ypass[side]
                for t in range(nt):
                    for k in range(2):
                        fill[k, t] += coefficients * ebuf[side, other, t, k:k + 1]

    solved = x_solve(
        lambda t: jnp.concatenate([fill[0, t], fill[1, t]], axis=0), xw, xpass, xthrough, nt
    )
    for t in range(nt):
        sz_ref[0, t] = solved[t][:yc]
        sz_ref[1, t] = solved[t][yc:]

    for side, to in ((0, up_row), (1, down_row)):
        @pl.when(to)
        def _():
            halo(side).wait_send()

    for k in range(nk):
        @pl.when(has_high)
        def _():
            z_copy(0, k).wait_send()

        @pl.when(has_low)
        def _():
            z_copy(1, k).wait_send()

    for other in range(nr):
        for side, there in ((0, other > row), (1, other < row)):
            @pl.when(there)
            def _():
                y_copy(side, other, row).wait_send()
                e_copy(side, other, row).wait_send()


def finish_kernel(planes, base, sy_ref, sz_ref, zpass, ypass, out_ref):
    nt = base.shape[0]
    for p in range(planes):
        z = pl.program_id(0) * planes + p
        zb, za = zpass[0, pl.ds(z, 1)], zpass[1, pl.ds(z, 1)]
        for t in range(nt):
            value = base[t, z] + (ypass[0] * sy_ref[0, t, pl.ds(z, 1)] + ypass[1] * sy_ref[1, t, pl.ds(z, 1)])
            value = value + (zb * sz_ref[0, t] + za * sz_ref[1, t])
            out_ref[p, :, t * LANES:(t + 1) * LANES] = value


def body(u, reaction, x_faces, y_faces, z_faces, x_inverse, y_inverse, z_inverse):
    zc, yc, nx = u.shape
    nr, nc = lax.axis_size("row"), lax.axis_size("col")
    f32, bf16 = jnp.float32, jnp.bfloat16
    nt, nk = nx // LANES, yc // 8
    bx = 256
    nb = nx // bx
    planes = next(p for p in (2, 1) if zc % p == 0)
    length = -(-max(x_faces.shape[0], y_faces.shape[0], z_faces.shape[0]) // LANES) * LANES
    hbm = pl.BlockSpec(memory_space=pltpu.HBM)
    vmem = pl.BlockSpec(memory_space=pltpu.VMEM)
    there = functools.partial(pltpu.with_memory_space_constraint, memory_space=pltpu.HBM)

    def on_chip(*shape, dtype=f32):
        return pltpu.VMEM(shape, dtype)

    dma = pltpu.SemaphoreType.DMA
    base, sy, sz, zpass, ypass = pl.pallas_call(
        functools.partial(main_kernel, nr, nc, planes),
        in_specs=[hbm] * 5,
        out_specs=[vmem] * 5,
        out_shape=[
            on_chip(nt, zc, yc, LANES),
            on_chip(2, nt, zc, LANES),
            on_chip(2, nt, yc, LANES),
            on_chip(2, zc, LANES),
            on_chip(2, yc, LANES),
        ],
        scratch_shapes=[
            on_chip(3, 8, length),
            on_chip(nt, zc, yc + 16, LANES),
            on_chip(2, nt, zc, LANES),
            on_chip(2, nt, zc, LANES),
            on_chip(nt, yc, LANES),
            on_chip(2, nt, LANES),
            on_chip(2, yc, LANES),
            on_chip(4, zc, LANES),
            on_chip(8, nx),
            on_chip(nb, 3 * bx, bx, dtype=bf16),
            on_chip(2, nt, LANES),
            on_chip(2, nb, LANES),
            on_chip(yc, 3 * yc, dtype=bf16),
            on_chip(2, nr, LANES),
            on_chip(nt, yc, LANES),
            on_chip(2, nk, nt, 8, LANES),
            on_chip(2, nk, nt, 8, LANES),
            on_chip(2, nk, nt, 8, LANES),
            on_chip(2, nt, zc, LANES),
            on_chip(2, nr, nt, zc, LANES),
            on_chip(2, nt, 2, LANES),
            on_chip(2, nr, nt, 2, LANES),
            on_chip(2, nt, yc, LANES),
            dma((3,)), dma((nt,)), dma((nk, nt)), dma((2,)), dma((2,)), dma((2, nk)), dma((2, nk)),
            dma((2, nr)), dma((2, nr)), dma((2, nr)), dma((2, nr)),
        ],
        compiler_params=pltpu.CompilerParams(
            collective_id=0, has_side_effects=True, vmem_limit_bytes=MAIN_VMEM
        ),
    )(there(x_faces[None]), there(y_faces[None]), there(z_faces[None]), there(u), there(reaction))

    last = next(p for p in (4, 2, 1) if zc % p == 0)
    return pl.pallas_call(
        functools.partial(finish_kernel, last),
        grid=(zc // last,),
        in_specs=[vmem] * 5,
        out_specs=pl.BlockSpec((last, yc, nx), lambda step: (step, 0, 0)),
        out_shape=jax.ShapeDtypeStruct((zc, yc, nx), f32),
        compiler_params=pltpu.CompilerParams(vmem_limit_bytes=LAST_VMEM),
    )(base, sy, sz, zpass, ypass)


def solution(mesh):
    in_specs = (P("col", "row", None), P("col", "row", None), P(), P(), P(), P(), P(), P())
    out_specs = P("col", "row", None)
    return jax.shard_map(body, mesh=mesh, in_specs=in_specs, out_specs=out_specs, check_vma=False)
```

time: 61.8 us -> 53.4 us (0.86)
  Pallas kernels: 59.5 us -> 53.2 us
  local copies, waits for them, and re-layouts: 2.04 us -> 0 us
    pallas_call x3 -> x1, Pallas kernels: 52.4 us -> 47.8 us  [body(): pl.pallas_call(functools.partial(main_kernel, nr, nc, planes), in_specs=[...]
    unnamed x6 -> x0, local copies, waits for them, and re-layouts: 2.04 us -> none
    pallas_call x1, Pallas kernels: 7.12 us -> 5.41 us  [body(): pl.pallas_call(functools.partial(finish_kernel, last), grid=(zc // last,)...]
where the time goes in v1:
time: 53.4 us; the launch traced here: 53.2 us
  Pallas kernels  53.2 us (100%)
    pallas_call x1, Pallas kernels, body(): pl.pallas_call(functools.partial(main_kernel, nr, nc, planes), in_specs=[...  47.8 us
    pallas_call x1, Pallas kernels, body(): pl.pallas_call(functools.partial(finish_kernel, last), grid=(zc // last,)...  5.41 us

profile of v1, /device:TPU:0, one launch (start us, length us, event | category | flops | bytes accessed | tf_op | source)
XLA Modules:
  0.0 53.2 jit_solution(13232000156516567511)
XLA Ops:
  0.0 47.8 %shard_map.55 = (f32[8,32,64,128]{3,2,1,0:T(8,128)S(1)}, f32[2,8,32,128]{3,2,1,0:T(8,128)S(1)}, f32[2,8,64,128]{3,2,1,0:T(8,128)S(1)}, f32[2,32,128]{2,1,0:T(8,128)S(1)}, f32[2,64,128]{2,1,0:T(8,128)S(1)}) custom-call(f32[1,1024]{1,0:T(1,128)} %bitcast.3, f32[1,256]{1,0:T(1,128)} %bitcast.4, f32[1,256]{1,0:T(1,128)} %bitcast.5, f32[32,64,1024]{2,1,0:T(8,128)} %field_ref.1, ...), custom_call_target="tpu_custom_call" | custom-call | tf_op jit(solution)/shard_map/pallas_call | solution.py:579
  47.8 5.4 %shard_map.56 = f32[32,64,1024]{2,1,0:T(8,128)} custom-call(f32[8,32,64,128]{3,2,1,0:T(8,128)S(1)} %get-tuple-element.10.base, f32[2,8,32,128]{3,2,1,0:T(8,128)S(1)} %get-tuple-element.11.sy_ref, f32[2,8,64,128]{3,2,1,0:T(8,128)S(1)} %get-tuple-element.12.sz_ref, f32[2,32,128]{2,1,0:T(8,128)S(1)} %get-tuple-element.13.zpass, ...), custom_call_target="tpu_custom_call" | custom-call | tf_op jit(solution)/shard_map/pallas_call | solution.py:623

commit v2 on v1

--- a/solution.py
+++ b/solution.py
@@ -13,6 +13,8 @@
 LANES = 128
 MAIN_VMEM = 24 * 1024 * 1024
 LAST_VMEM = 12 * 1024 * 1024
+FIRST_NS, HOP_NS, CHUNK_NS = 1100, 2100, 250
+SECOND_NS, TABLE_NS, THIRD_NS = 280, 180, 820
 
 
 def shifted(a, by, fill):
@@ -102,12 +104,12 @@
 
 
 def main_kernel(
-    nr, nc, planes, xf_hbm, yf_hbm, zf_hbm, field_ref, rea_ref,
+    nr, nc, planes, wide, xf_hbm, yf_hbm, zf_hbm, field_ref, rea_ref,
     base, sy_ref, sz_ref, zpass, ypass,
     faces, u, edges, yhalo, coef, xface, yface, ztab, xline, xw, xpass, xthrough, ym, weights,
-    vprev, zedge, zsend, zbuf, ye, ybuf, esend, ebuf, fill,
-    face_sem, u_sem, rea_sem, hsend, hrecv, zsend_sem, zrecv_sem,
-    ysend_sem, yrecv_sem, esend_sem, erecv_sem,
+    vprev, zedge, zsend, zbuf, pbuf, through, ye, ybuf, esend, ebuf, fill,
+    face_sem, u_sem, rea_sem, hsend, hrecv, zsend_sem, zrecv_sem, psend_sem, precv_sem,
+    fsend_sem, frecv_sem, ysend_sem, yrecv_sem, esend_sem, erecv_sem,
 ):
     row, col = lax.axis_index("row"), lax.axis_index("col")
     nt, zc, yc, _ = base.shape
@@ -137,23 +139,32 @@
         copy.start()
 
     up_row, down_row = row < nr - 1, row > 0
-    has_low, has_high = col > 0, col < nc - 1
+    core, chip, chips = lax.rem(col, 2), col // 2, nc // 2
+    mine, theirs = 1 - core, core
+    far = jnp.where(core == 1, chip, chips - 1 - chip)
+    chained, chains, fed = far > 0, far < chips - 1, far < chips - 1
+    partner, following = col + 1 - 2 * core, col + 2 * (2 * core - 1)
+    below, beyond = col >= 2, col < nc - 2
     barrier = pltpu.get_barrier_semaphore()
     for other in range(nr):
         @pl.when(other != row)
         def _():
             pl.semaphore_signal(barrier, inc=1, device_id=(other, col), device_id_type=MESH)
 
-    @pl.when(has_low)
+    pl.semaphore_signal(barrier, inc=1, device_id=(row, partner), device_id_type=MESH)
+
+    @pl.when(below)
     def _():
-        pl.semaphore_signal(barrier, inc=1, device_id=(row, col - 1), device_id_type=MESH)
-
-    @pl.when(has_high)
+        pl.semaphore_signal(barrier, inc=1, device_id=(row, col - 2), device_id_type=MESH)
+
+    @pl.when(beyond)
     def _():
-        pl.semaphore_signal(barrier, inc=1, device_id=(row, col + 1), device_id_type=MESH)
+        pl.semaphore_signal(barrier, inc=1, device_id=(row, col + 2), device_id_type=MESH)
 
     vprev[...] = jnp.zeros_like(vprev)
-    for side, source, there in ((0, has_low, down_row), (1, has_high, up_row)):
+    for side, there in ((0, down_row), (1, up_row)):
+        source = chip > 0 if side == 0 else chip < chips - 1
+
         @pl.when(jnp.logical_not(source))
         def _():
             zbuf[side] = jnp.zeros(zbuf.shape[1:], f32)
@@ -217,6 +228,11 @@
         ztab[i] = lanes_of(turned[:zc, i:i + 1])
     for i in range(2):
         zpass[i] = lanes_of(turned[:zc, 4 + i:5 + i])
+    _, _, _, ponward, pbackward = passes(2, partner * zc, zc)
+    here_on = jnp.where(core == 1, onward[:, zc - 1:zc], backward[:, 0:1])
+    first_on = jnp.where(core == 1, ponward[:, zc - 1:zc], pbackward[:, 0:1])
+    for i, value in enumerate((here_on, first_on, here_on * first_on)):
+        through[i:i + 1] = lanes_of(value)
 
     y0 = row * yc
     sums, up_first, down_last, onward, backward = passes(1, y0, yc)
@@ -231,7 +247,8 @@
         coef[t] = ycoef - around[0:1, t * LANES:(t + 1) * LANES]
     block = block_of_inverse(own(diag, 1, y0)[:, :LANES], sums[:, :LANES], LANES)[:yc, :yc]
     high, low = split(block)
-    ym[...] = jnp.concatenate([high, high, low], axis=1)
+    ym[0:yc] = jnp.concatenate([high, high], axis=1)
+    ym[yc:2 * yc] = jnp.concatenate([low, jnp.zeros_like(low)], axis=1)
     for other in range(nr):
         last, first = (other + 1) * yc - 1, other * yc
         value = jnp.exp(jnp.minimum(up_first - ups[1:2, last:last + 1], 0.0))
@@ -262,7 +279,7 @@
         return 0
 
     lax.fori_loop(0, zc, take_edges, 0, unroll=4 if zc % 4 == 0 else 1)
-    pl.semaphore_wait(barrier, nr - 1 + has_low.astype(jnp.int32) + has_high.astype(jnp.int32))
+    pl.semaphore_wait(barrier, nr + below.astype(jnp.int32) + beyond.astype(jnp.int32))
 
     def halo(side):
         return pltpu.make_async_remote_copy(
@@ -276,32 +293,52 @@
         def _():
             halo(side).start()
 
-    def z_copy(side, k):
+    def pair_copy(k):
         return pltpu.make_async_remote_copy(
-            src_ref=zsend.at[side, k], dst_ref=zbuf.at[side, k],
-            send_sem=zsend_sem.at[side, k], recv_sem=zrecv_sem.at[side, k],
-            device_id=(row, col + (1 - 2 * side)), device_id_type=MESH,
-        )
-
-    far = (col, nc - 1 - col)
-
-    def relay(side, k):
-        source, target = (has_low, has_high) if side == 0 else (has_high, has_low)
-        at_row = zc - 1 if side == 0 else 0
-
-        @pl.when(source)
-        def _():
-            z_copy(side, k).wait_recv()
-
-        @pl.when(target)
-        def _():
-            through = zpass[side, at_row:at_row + 1]
+            src_ref=zedge.at[theirs, k], dst_ref=pbuf.at[k],
+            send_sem=psend_sem.at[k], recv_sem=precv_sem.at[k],
+            device_id=(row, partner), device_id_type=MESH,
+        )
+
+    def chain_copy(k):
+        return pltpu.make_async_remote_copy(
+            src_ref=zsend.at[k], dst_ref=zbuf.at[mine, k],
+            send_sem=zsend_sem.at[k], recv_sem=zrecv_sem.at[k],
+            device_id=(row, following), device_id_type=MESH,
+        )
+
+    def forward_copy(k):
+        return pltpu.make_async_remote_copy(
+            src_ref=zbuf.at[mine, k], dst_ref=zbuf.at[mine, k],
+            send_sem=fsend_sem.at[k], recv_sem=frecv_sem.at[k],
+            device_id=(row, partner), device_id_type=MESH,
+        )
+
+    def relay(k):
+        pair_copy(k).wait_recv()
+
+        @pl.when(chained)
+        def _():
+            chain_copy(k).wait_recv()
+            forward_copy(k).start()
+
+        @pl.when(chains)
+        def _():
+            own_on, both_on = through[0:1], through[2:3]
             for t in range(nt):
-                zsend[side, k, t] = zedge[side, k, t] + through * zbuf[side, k, t]
-            z_copy(side, k).start()
+                value = zedge[mine, k, t] + own_on * pbuf[k, t]
+                zsend[k, t] = value + both_on * zbuf[mine, k, t]
+            chain_copy(k).start()
+
+    def chunk_at(j):
+        return lax.rem(j + 1, nk)
+
+    lag = (5 * far + 1) // 2
 
     lane = lax.broadcasted_iota(jnp.int32, (8, LANES), 1)
     group = min(nt, 8)
+
+    long = next(n for n in (16, 8, 4, 2, 1) if zc % n == 0)
 
     def first_pass(i, _):
         k = lax.rem(i + 1, nk)
@@ -353,40 +390,43 @@
                 return new_tops, new_lows
 
             zero = [jnp.zeros((8, LANES), f32) for _ in tiles]
-            tops, lows = lax.fori_loop(0, zc, one, (zero, zero), unroll=2 if zc % 2 == 0 else 1)
+            tops, lows = lax.fori_loop(0, zc, one, (zero, zero), unroll=long)
             for j, t in enumerate(tiles):
                 zedge[0, k, t] = tops[j]
                 zedge[1, k, t] = lows[j]
 
-        for side in (0, 1):
-            turn = i - 2 * far[side]
-
-            @pl.when(turn >= 0)
-            def _():
-                relay(side, lax.rem(turn + 1, nk))
+        pair_copy(k).start()
+        turn = i - 1 - lag
+
+        @pl.when(turn >= 0)
+        def _():
+            relay(chunk_at(turn))
 
         return 0
 
     lax.fori_loop(0, nk, first_pass, 0)
 
-    def slot_of(d):
-        return 5 * ((d + 1) // 2) + 9 * (d // 2)
-
-    def relays(slot):
-        for side in (0, 1):
-            d = far[side]
-            turn = slot - (slot_of(d) - (nk - 1))
-
-            @pl.when((turn >= jnp.maximum(nk - 2 * d, 0)) & (turn < nk))
-            def _():
-                relay(side, lax.rem(turn + 1, nk))
+    due = FIRST_NS + HOP_NS * far
+    begun = jnp.maximum(nk - 1 - lag, 0)
+
+    def count(now):
+        ahead = (jnp.maximum(now - due + nk * CHUNK_NS, 0)) // CHUNK_NS
+        return jnp.clip(ahead, begun, nk)
+
+    def relays(since, now):
+        def one(j, _):
+            relay(chunk_at(j))
+            return 0
+
+        lax.fori_loop(count(since), count(now), one, 0)
 
     per = 256 // LANES
     steps = zc // planes
 
     def y_solve(tiles):
         high, low = split(jnp.concatenate(tiles, axis=1))
-        return dot(ym[...], jnp.concatenate([high, low, high], axis=0))
+        both = dot(ym[...], jnp.concatenate([high, low], axis=0))
+        return both[:yc] + both[yc:]
 
     def second_pass(slot, _):
         for p in range(planes):
@@ -405,10 +445,11 @@
                     base[t, z] = part
                     ye[0, t, pl.ds(z, 1)] = part[0:1]
                     ye[1, t, pl.ds(z, 1)] = part[yc - 1:yc]
-        relays(slot)
+        relays(SECOND_NS * slot, SECOND_NS * (slot + 1))
         return 0
 
     lax.fori_loop(0, steps, second_pass, 0)
+    now = SECOND_NS * steps
 
     def y_copy(side, other, slot):
         return pltpu.make_async_remote_copy(
@@ -442,40 +483,48 @@
             xpass[1, t:t + 1] = back[:, i * LANES:(i + 1) * LANES]
         xthrough[0, b:b + 1] = lanes_of(ahead[:, bx - 1:bx])
         xthrough[1, b:b + 1] = lanes_of(back[:, 0:1])
-
-    def third_pass(slot, _):
-        zs = [slot * planes + p for p in range(planes)]
+        relays(now, now + TABLE_NS)
+        now += TABLE_NS
+
+    def third(slot):
+        zs = [slot * wide + p for p in range(wide)]
         solved = x_solve(
             lambda t: jnp.concatenate([base[t, z] for z in zs], axis=0), xw, xpass, xthrough, nt
         )
         for t in range(nt):
             for p, z in enumerate(zs):
                 base[t, z] = u[t, z, 8:8 + yc] + solved[t][p * yc:(p + 1) * yc]
-        relays(steps + slot)
+
+    def third_pass(slot, _):
+        third(slot)
+        relays(now + THIRD_NS * slot, now + THIRD_NS * (slot + 1))
         return 0
 
-    lax.fori_loop(0, steps, third_pass, 0)
-
-    def tail(slot, _):
-        relays(slot)
-        return 0
-
-    most = slot_of(nc - 1) + 1
-    lax.fori_loop(2 * steps, max(2 * steps, most), tail, 0)
-
-    for k in range(2):
+    early = (zc // wide + 1) // 2
+    lax.fori_loop(0, early, third_pass, 0)
+    relays(now + THIRD_NS * early, 1 << 30)
+
+    @pl.when(fed)
+    def _():
+        for k in range(nk):
+            forward_copy(k).wait_recv()
+
+    for which in range(2):
+        k = theirs if which else mine
         for b in range(nt // per):
-            tiles = [
-                jnp.concatenate([zbuf[k, j, t] for j in range(nk)], axis=0)
-                for t in range(b * per, (b + 1) * per)
-            ]
+            tiles = []
+            for t in range(b * per, (b + 1) * per):
+                pieces = [zbuf[k, j, t] for j in range(nk)]
+                if not which:
+                    pieces = [pbuf[j, t] + through[1:2] * pieces[j] for j in range(nk)]
+                tiles.append(jnp.concatenate(pieces, axis=0))
             solved = y_solve(tiles)
             for i in range(per):
                 t = b * per + i
                 part = solved[:, i * LANES:(i + 1) * LANES]
                 fill[k, t] = part
-                esend[0, t, k:k + 1] = part[yc - 1:yc]
-                esend[1, t, k:k + 1] = part[0:1]
+                esend[0, t, pl.ds(k, 1)] = part[yc - 1:yc]
+                esend[1, t, pl.ds(k, 1)] = part[0:1]
 
     def e_copy(side, other, slot):
         return pltpu.make_async_remote_copy(
@@ -492,6 +541,12 @@
         @pl.when(other < row)
         def _():
             e_copy(1, other, row).start()
+
+    def last_pass(slot, _):
+        third(slot)
+        return 0
+
+    lax.fori_loop(early, zc // wide, last_pass, 0)
 
     sy_ref[...] = jnp.zeros_like(sy_ref)
     for other in range(nr):
@@ -501,13 +556,6 @@
                 y_copy(side, other, other).wait_recv()
                 for t in range(nt):
                     sy_ref[side, t] += weights[side, other:other + 1] * ybuf[side, other, t]
-
-    solved = x_solve(
-        lambda t: jnp.concatenate([sy_ref[0, t], sy_ref[1, t]], axis=0), xw, xpass, xthrough, nt
-    )
-    for t in range(nt):
-        sy_ref[0, t] = solved[t][:zc]
-        sy_ref[1, t] = solved[t][zc:]
 
     for other in range(nr):
         for side, there in ((0, other < row), (1, other > row)):
@@ -520,11 +568,14 @@
                         fill[k, t] += coefficients * ebuf[side, other, t, k:k + 1]
 
     solved = x_solve(
-        lambda t: jnp.concatenate([fill[0, t], fill[1, t]], axis=0), xw, xpass, xthrough, nt
+        lambda t: jnp.concatenate([fill[0, t], fill[1, t], sy_ref[0, t], sy_ref[1, t]], axis=0),
+        xw, xpass, xthrough, nt,
     )
     for t in range(nt):
         sz_ref[0, t] = solved[t][:yc]
-        sz_ref[1, t] = solved[t][yc:]
+        sz_ref[1, t] = solved[t][yc:2 * yc]
+        sy_ref[0, t] = solved[t][2 * yc:2 * yc + zc]
+        sy_ref[1, t] = solved[t][2 * yc + zc:]
 
     for side, to in ((0, up_row), (1, down_row)):
         @pl.when(to)
@@ -532,13 +583,15 @@
             halo(side).wait_send()
 
     for k in range(nk):
-        @pl.when(has_high)
-        def _():
-            z_copy(0, k).wait_send()
-
-        @pl.when(has_low)
-        def _():
-            z_copy(1, k).wait_send()
+        pair_copy(k).wait_send()
+
+        @pl.when(chained)
+        def _():
+            forward_copy(k).wait_send()
+
+        @pl.when(chains)
+        def _():
+            chain_copy(k).wait_send()
 
     for other in range(nr):
         for side, there in ((0, other > row), (1, other < row)):
@@ -548,15 +601,33 @@
                 e_copy(side, other, row).wait_send()
 
 
-def finish_kernel(planes, base, sy_ref, sz_ref, zpass, ypass, out_ref):
-    nt = base.shape[0]
-    for p in range(planes):
-        z = pl.program_id(0) * planes + p
-        zb, za = zpass[0, pl.ds(z, 1)], zpass[1, pl.ds(z, 1)]
-        for t in range(nt):
-            value = base[t, z] + (ypass[0] * sy_ref[0, t, pl.ds(z, 1)] + ypass[1] * sy_ref[1, t, pl.ds(z, 1)])
-            value = value + (zb * sz_ref[0, t] + za * sz_ref[1, t])
-            out_ref[p, :, t * LANES:(t + 1) * LANES] = value
+def finish_kernel(planes, base, sy_ref, sz_ref, zpass, ypass, out_ref, staged, sem):
+    nt, zc = base.shape[0], base.shape[1]
+
+    def out_copy(i):
+        part = pl.ds(i * planes, planes)
+        return pltpu.make_async_copy(staged.at[part], out_ref.at[part], sem.at[i])
+
+    def one(i, _):
+        for p in range(planes):
+            z = i * planes + p
+            zb, za = zpass[0, pl.ds(z, 1)], zpass[1, pl.ds(z, 1)]
+            for t in range(nt):
+                value = base[t, z] + (
+                    ypass[0] * sy_ref[0, t, pl.ds(z, 1)] + ypass[1] * sy_ref[1, t, pl.ds(z, 1)]
+                )
+                value = value + (zb * sz_ref[0, t] + za * sz_ref[1, t])
+                staged[z, :, t * LANES:(t + 1) * LANES] = value
+        out_copy(i).start()
+        return 0
+
+    lax.fori_loop(0, zc // planes, one, 0)
+
+    def end(i, _):
+        out_copy(i).wait()
+        return 0
+
+    lax.fori_loop(0, zc // planes, end, 0)
 
 
 def body(u, reaction, x_faces, y_faces, z_faces, x_inverse, y_inverse, z_inverse):
@@ -567,6 +638,7 @@
     bx = 256
     nb = nx // bx
     planes = next(p for p in (2, 1) if zc % p == 0)
+    wide = next(p for p in (4, 2, 1) if zc % p == 0)
     length = -(-max(x_faces.shape[0], y_faces.shape[0], z_faces.shape[0]) // LANES) * LANES
     hbm = pl.BlockSpec(memory_space=pltpu.HBM)
     vmem = pl.BlockSpec(memory_space=pltpu.VMEM)
@@ -577,7 +649,7 @@
 
     dma = pltpu.SemaphoreType.DMA
     base, sy, sz, zpass, ypass = pl.pallas_call(
-        functools.partial(main_kernel, nr, nc, planes),
+        functools.partial(main_kernel, nr, nc, planes, wide),
         in_specs=[hbm] * 5,
         out_specs=[vmem] * 5,
         out_shape=[
@@ -600,32 +672,34 @@
             on_chip(nb, 3 * bx, bx, dtype=bf16),
             on_chip(2, nt, LANES),
             on_chip(2, nb, LANES),
-            on_chip(yc, 3 * yc, dtype=bf16),
+            on_chip(2 * yc, 2 * yc, dtype=bf16),
             on_chip(2, nr, LANES),
             on_chip(nt, yc, LANES),
             on_chip(2, nk, nt, 8, LANES),
+            on_chip(nk, nt, 8, LANES),
             on_chip(2, nk, nt, 8, LANES),
-            on_chip(2, nk, nt, 8, LANES),
+            on_chip(nk, nt, 8, LANES),
+            on_chip(8, LANES),
             on_chip(2, nt, zc, LANES),
             on_chip(2, nr, nt, zc, LANES),
             on_chip(2, nt, 2, LANES),
             on_chip(2, nr, nt, 2, LANES),
             on_chip(2, nt, yc, LANES),
-            dma((3,)), dma((nt,)), dma((nk, nt)), dma((2,)), dma((2,)), dma((2, nk)), dma((2, nk)),
-            dma((2, nr)), dma((2, nr)), dma((2, nr)), dma((2, nr)),
+            dma((3,)), dma((nt,)), dma((nk, nt)), dma((2,)), dma((2,)), dma((nk,)), dma((nk,)), dma((nk,)),
+            dma((nk,)), dma((nk,)), dma((nk,)), dma((2, nr)), dma((2, nr)), dma((2, nr)), dma((2, nr)),
         ],
         compiler_params=pltpu.CompilerParams(
             collective_id=0, has_side_effects=True, vmem_limit_bytes=MAIN_VMEM
         ),
     )(there(x_faces[None]), there(y_faces[None]), there(z_faces[None]), there(u), there(reaction))
 
-    last = next(p for p in (4, 2, 1) if zc % p == 0)
+    last = next(p for p in (2, 1) if zc % p == 0)
     return pl.pallas_call(
         functools.partial(finish_kernel, last),
-        grid=(zc // last,),
         in_specs=[vmem] * 5,
-        out_specs=pl.BlockSpec((last, yc, nx), lambda step: (step, 0, 0)),
+        out_specs=hbm,
         out_shape=jax.ShapeDtypeStruct((zc, yc, nx), f32),
+        scratch_shapes=[on_chip(zc, yc, nx), dma((zc // last,))],
         compiler_params=pltpu.CompilerParams(vmem_limit_bytes=LAST_VMEM),
     )(base, sy, sz, zpass, ypass)
 

time: 53.4 us -> 39.2 us (0.73)
  Pallas kernels: 53.2 us -> 39 us
    pallas_call x2, Pallas kernels: 53.2 us -> 39 us  [the longest x1 35.5 us: body(): pl.pallas_call(functools.partial(main_kernel, nr, nc, planes, wide), in_s...]
where the time goes in v2:
time: 39.2 us; the launch traced here: 39 us
  Pallas kernels  39 us (99%)
    pallas_call x1, Pallas kernels, body(): pl.pallas_call(functools.partial(main_kernel, nr, nc, planes, wide), in_s...  35.5 us
    pallas_call x1, Pallas kernels, body(): pl.pallas_call(functools.partial(finish_kernel, last), in_specs=[vmem] *...  3.56 us

profile of v2, /device:TPU:0, one launch (start us, length us, event | category | flops | bytes accessed | tf_op | source)
XLA Modules:
  0.0 39.0 jit_solution(10620979455795386928)
XLA Ops:
  0.0 35.5 %shard_map.55 = (f32[8,32,64,128]{3,2,1,0:T(8,128)S(1)}, f32[2,8,32,128]{3,2,1,0:T(8,128)S(1)}, f32[2,8,64,128]{3,2,1,0:T(8,128)S(1)}, f32[2,32,128]{2,1,0:T(8,128)S(1)}, f32[2,64,128]{2,1,0:T(8,128)S(1)}) custom-call(f32[1,1024]{1,0:T(1,128)} %bitcast.3, f32[1,256]{1,0:T(1,128)} %bitcast.4, f32[1,256]{1,0:T(1,128)} %bitcast.5, f32[32,64,1024]{2,1,0:T(8,128)} %field_ref.1, ...), custom_call_target="tpu_custom_call" | custom-call | tf_op jit(solution)/shard_map/pallas_call | solution.py:651
  35.5 3.6 %shard_map.56 = f32[32,64,1024]{2,1,0:T(8,128)} custom-call(f32[8,32,64,128]{3,2,1,0:T(8,128)S(1)} %get-tuple-element.10.base, f32[2,8,32,128]{3,2,1,0:T(8,128)S(1)} %get-tuple-element.11.sy_ref, f32[2,8,64,128]{3,2,1,0:T(8,128)S(1)} %get-tuple-element.12.sz_ref, f32[2,32,128]{2,1,0:T(8,128)S(1)} %get-tuple-element.13.zpass, ...), custom_call_target="tpu_custom_call" | custom-call | tf_op jit(solution)/shard_map/pallas_call | solution.py:697

commit v3 on v2

--- a/solution.py
+++ b/solution.py
@@ -104,7 +104,7 @@
 
 
 def main_kernel(
-    nr, nc, planes, wide, xf_hbm, yf_hbm, zf_hbm, field_ref, rea_ref,
+    nr, nc, planes, wide, u_bands, xf_hbm, yf_hbm, zf_hbm, field_ref, rea_ref,
     base, sy_ref, sz_ref, zpass, ypass,
     faces, u, edges, yhalo, coef, xface, yface, ztab, xline, xw, xpass, xthrough, ym, weights,
     vprev, zedge, zsend, zbuf, pbuf, through, ye, ybuf, esend, ebuf, fill,
@@ -129,14 +129,33 @@
             faces[i, 0:1, a.shape[1]:] = jnp.zeros((1, length - a.shape[1]), f32)
     for copy in face_copies:
         copy.start()
-    u_copies = [
-        pltpu.make_async_copy(
-            field_ref.at[:, :, pl.ds(t * LANES, LANES)], u.at[t, :, pl.ds(8, yc)], u_sem.at[t]
-        )
-        for t in range(nt)
-    ]
-    for copy in u_copies:
-        copy.start()
+    bands = len(u_bands)
+    first_row = [sum(u_bands[:i]) for i in range(bands)]
+
+    def u_copy(i, t):
+        return pltpu.make_async_copy(
+            field_ref.at[:, pl.ds(first_row[i], u_bands[i]), pl.ds(t * LANES, LANES)],
+            u.at[t, :, pl.ds(8 + first_row[i], u_bands[i])], u_sem.at[i, t],
+        )
+
+    def rea_copy(k, t):
+        rows = pl.ds(k * 8 if isinstance(k, int) else pl.multiple_of(k * 8, 8), 8)
+        return pltpu.make_async_copy(
+            rea_ref.at[:, rows, pl.ds(t * LANES, LANES)], base.at[t, :, rows], rea_sem.at[k, t]
+        )
+
+    waiting = [(k + 1) % nk for k in range(nk)]
+    for i in [0, bands - 1] + list(range(1, bands - 1)) if bands > 1 else [0]:
+        for t in range(nt):
+            u_copy(i, t).start()
+        if i >= min(1, bands - 1) and i < bands - 1 or bands <= 2 and i == bands - 1:
+            for k in waiting[:2]:
+                for t in range(nt):
+                    rea_copy(k, t).start()
+            waiting = waiting[2:]
+    for k in waiting:
+        for t in range(nt):
+            rea_copy(k, t).start()
 
     up_row, down_row = row < nr - 1, row > 0
     core, chip, chips = lax.rem(col, 2), col // 2, nc // 2
@@ -247,8 +266,7 @@
         coef[t] = ycoef - around[0:1, t * LANES:(t + 1) * LANES]
     block = block_of_inverse(own(diag, 1, y0)[:, :LANES], sums[:, :LANES], LANES)[:yc, :yc]
     high, low = split(block)
-    ym[0:yc] = jnp.concatenate([high, high], axis=1)
-    ym[yc:2 * yc] = jnp.concatenate([low, jnp.zeros_like(low)], axis=1)
+    ym[...] = jnp.concatenate([high, high, low], axis=1)
     for other in range(nr):
         last, first = (other + 1) * yc - 1, other * yc
         value = jnp.exp(jnp.minimum(up_first - ups[1:2, last:last + 1], 0.0))
@@ -256,21 +274,9 @@
         value = jnp.exp(jnp.minimum(downs_before[1:2, first:first + 1] - down_last, 0.0))
         weights[1, other:other + 1] = lanes_of(value)
 
-    def rea_copy(k, t):
-        rows = pl.ds(pl.multiple_of(k * 8, 8), 8)
-        return pltpu.make_async_copy(
-            rea_ref.at[:, rows, pl.ds(t * LANES, LANES)], base.at[t, :, rows], rea_sem.at[k, t]
-        )
-
-    def start_rea(i, _):
-        k = lax.rem(i + 1, nk)
+    for i in sorted({0, bands - 1}):
         for t in range(nt):
-            rea_copy(k, t).start()
-        return 0
-
-    lax.fori_loop(0, nk, start_rea, 0)
-    for copy in u_copies:
-        copy.wait()
+            u_copy(i, t).wait()
 
     def take_edges(z, _):
         for t in range(nt):
@@ -346,6 +352,12 @@
         rows = pl.ds(y, 8)
         for t in range(nt):
             rea_copy(k, t).wait()
+
+        for b in range(1, bands - 1):
+            @pl.when(i == max(first_row[b] // 8 - 2, 0))
+            def _():
+                for t in range(nt):
+                    u_copy(b, t).wait()
 
         @pl.when(i == nk - 2)
         def _():
@@ -425,8 +437,7 @@
 
     def y_solve(tiles):
         high, low = split(jnp.concatenate(tiles, axis=1))
-        both = dot(ym[...], jnp.concatenate([high, low], axis=0))
-        return both[:yc] + both[yc:]
+        return dot(ym[...], jnp.concatenate([high, low, high], axis=0))
 
     def second_pass(slot, _):
         for p in range(planes):
@@ -637,6 +648,7 @@
     nt, nk = nx // LANES, yc // 8
     bx = 256
     nb = nx // bx
+    u_bands = [16] * (yc // 16) if yc % 16 == 0 else [yc]
     planes = next(p for p in (2, 1) if zc % p == 0)
     wide = next(p for p in (4, 2, 1) if zc % p == 0)
     length = -(-max(x_faces.shape[0], y_faces.shape[0], z_faces.shape[0]) // LANES) * LANES
@@ -649,7 +661,7 @@
 
     dma = pltpu.SemaphoreType.DMA
     base, sy, sz, zpass, ypass = pl.pallas_call(
-        functools.partial(main_kernel, nr, nc, planes, wide),
+        functools.partial(main_kernel, nr, nc, planes, wide, u_bands),
         in_specs=[hbm] * 5,
         out_specs=[vmem] * 5,
         out_shape=[
@@ -672,7 +684,7 @@
             on_chip(nb, 3 * bx, bx, dtype=bf16),
             on_chip(2, nt, LANES),
             on_chip(2, nb, LANES),
-            on_chip(2 * yc, 2 * yc, dtype=bf16),
+            on_chip(yc, 3 * yc, dtype=bf16),
             on_chip(2, nr, LANES),
             on_chip(nt, yc, LANES),
             on_chip(2, nk, nt, 8, LANES),
@@ -685,7 +697,7 @@
             on_chip(2, nt, 2, LANES),
             on_chip(2, nr, nt, 2, LANES),
             on_chip(2, nt, yc, LANES),
-            dma((3,)), dma((nt,)), dma((nk, nt)), dma((2,)), dma((2,)), dma((nk,)), dma((nk,)), dma((nk,)),
+            dma((3,)), dma((len(u_bands), nt)), dma((nk, nt)), dma((2,)), dma((2,)), dma((nk,)), dma((nk,)), dma((nk,)),
             dma((nk,)), dma((nk,)), dma((nk,)), dma((2, nr)), dma((2, nr)), dma((2, nr)), dma((2, nr)),
         ],
         compiler_params=pltpu.CompilerParams(

time: 39.2 us -> 37.9 us (0.967)
  Pallas kernels: 39 us -> 37.7 us
    pallas_call x1, Pallas kernels: 35.5 us -> 34.2 us  [body(): pl.pallas_call(functools.partial(main_kernel, nr, nc, planes, wide, u_ban...]
where the time goes in v3:
time: 37.9 us; the launch traced here: 37.7 us
  Pallas kernels  37.7 us (99%)
    pallas_call x1, Pallas kernels, body(): pl.pallas_call(functools.partial(main_kernel, nr, nc, planes, wide, u_ban...  34.2 us
    pallas_call x1, Pallas kernels, body(): pl.pallas_call(functools.partial(finish_kernel, last), in_specs=[vmem] *...  3.56 us

profile of v3, /device:TPU:0, one launch (start us, length us, event | category | flops | bytes accessed | tf_op | source)
XLA Modules:
  0.0 37.7 jit_solution(1158790844504463630)
XLA Ops:
  0.0 34.2 %shard_map.55 = (f32[8,32,64,128]{3,2,1,0:T(8,128)S(1)}, f32[2,8,32,128]{3,2,1,0:T(8,128)S(1)}, f32[2,8,64,128]{3,2,1,0:T(8,128)S(1)}, f32[2,32,128]{2,1,0:T(8,128)S(1)}, f32[2,64,128]{2,1,0:T(8,128)S(1)}) custom-call(f32[1,1024]{1,0:T(1,128)} %bitcast.3, f32[1,256]{1,0:T(1,128)} %bitcast.4, f32[1,256]{1,0:T(1,128)} %bitcast.5, f32[32,64,1024]{2,1,0:T(8,128)} %field_ref.1, ...), custom_call_target="tpu_custom_call" | custom-call | tf_op jit(solution)/shard_map/pallas_call | solution.py:663
  34.2 3.6 %shard_map.56 = f32[32,64,1024]{2,1,0:T(8,128)} custom-call(f32[8,32,64,128]{3,2,1,0:T(8,128)S(1)} %get-tuple-element.10.base, f32[2,8,32,128]{3,2,1,0:T(8,128)S(1)} %get-tuple-element.11.sy_ref, f32[2,8,64,128]{3,2,1,0:T(8,128)S(1)} %get-tuple-element.12.sz_ref, f32[2,32,128]{2,1,0:T(8,128)S(1)} %get-tuple-element.13.zpass, ...), custom_call_target="tpu_custom_call" | custom-call | tf_op jit(solution)/shard_map/pallas_call | solution.py:709

commit v4 on v3

--- a/solution.py
+++ b/solution.py
@@ -11,7 +11,8 @@
 STEP = 1000.0
 MESH = pl.DeviceIdType.MESH
 LANES = 128
-MAIN_VMEM = 24 * 1024 * 1024
+TOGETHER = 4
+MAIN_VMEM = 32 * 1024 * 1024
 LAST_VMEM = 12 * 1024 * 1024
 FIRST_NS, HOP_NS, CHUNK_NS = 1100, 2100, 250
 SECOND_NS, TABLE_NS, THIRD_NS = 280, 180, 820
@@ -106,7 +107,7 @@
 def main_kernel(
     nr, nc, planes, wide, u_bands, xf_hbm, yf_hbm, zf_hbm, field_ref, rea_ref,
     base, sy_ref, sz_ref, zpass, ypass,
-    faces, u, edges, yhalo, coef, xface, yface, ztab, xline, xw, xpass, xthrough, ym, weights,
+    faces, u, edges, yhalo, coef, xface, yface, ztab, xline, xw, xpass, xthrough, ym, ysolve, along, weights,
     vprev, zedge, zsend, zbuf, pbuf, through, ye, ybuf, esend, ebuf, fill,
     face_sem, u_sem, rea_sem, hsend, hrecv, zsend_sem, zrecv_sem, psend_sem, precv_sem,
     fsend_sem, frecv_sem, ysend_sem, yrecv_sem, esend_sem, erecv_sem,
@@ -256,7 +257,35 @@
     y0 = row * yc
     sums, up_first, down_last, onward, backward = passes(1, y0, yc)
     ky, kyn, kya = own(lines, 1, y0), own(next_lines, 1, y0), own(around, 1, y0)
-    turned = columns([ky, kyn, 1.0 / scale - kya, onward, backward])
+    seg = yc // 8
+    place = lax.rem(at, seg)
+    yups, yups_before = own(ups, 1, y0), own(ups_before, 1, y0)
+    ydowns, ydowns_before = own(downs, 1, y0), own(downs_before, 1, y0)
+    begins, ends = yups_before, ydowns
+    for j in range(1, seg):
+        begins = jnp.where(place == j, pltpu.roll(yups_before, j, 1), begins)
+        ends = jnp.where(place == seg - 1 - j, pltpu.roll(ydowns, length - j, 1), ends)
+
+    def decay(a):
+        return jnp.exp(jnp.minimum(a, 0.0))
+
+    seg_over = jnp.where(place == seg - 1, own(diag, 1, y0), own(inverse, 1, y0))
+    seg_lines = [
+        seg_over,
+        jnp.where(place == 0, 0.0, own(here, 1, y0) * seg_over),
+        own(down, 1, y0),
+        jnp.where(at < seg, 0.0, decay(yups - begins)),
+        jnp.where(at >= yc - seg, 0.0, decay(ends - ydowns_before)),
+    ]
+    for d in (1, 2, 4):
+        value = decay(yups - pltpu.roll(yups, d * seg, 1))
+        seg_lines.append(jnp.where(at < d * seg, 0.0, value))
+    for d in (1, 2, 4):
+        value = decay(pltpu.roll(ydowns_before, length - d * seg, 1) - ydowns_before)
+        seg_lines.append(jnp.where(at >= yc - d * seg, 0.0, value))
+    turned = columns([ky, kyn, 1.0 / scale - kya, onward, backward] + seg_lines)
+    for i in range(len(seg_lines)):
+        ysolve[i] = lanes_of(turned[:yc, 5 + i:6 + i])
     yface[0] = lanes_of(turned[:yc, 0:1])
     yface[1] = lanes_of(turned[:yc, 1:2])
     ypass[0] = lanes_of(turned[:yc, 3:4])
@@ -439,21 +468,64 @@
         high, low = split(jnp.concatenate(tiles, axis=1))
         return dot(ym[...], jnp.concatenate([high, low, high], axis=0))
 
+    def segments(j):
+        return pl.ds(j, 8, stride=seg)
+
+    def y_lines(lines):
+        w = [[] for _ in lines]
+        for j in range(seg):
+            over, into = ysolve[0, segments(j)], ysolve[1, segments(j)]
+            for i, (_, _, ready) in enumerate(lines):
+                value = over * ready[j]
+                w[i].append(value + into * w[i][-1] if j else value)
+        v = [[a[-1]] for a in w]
+        for j in range(seg - 2, -1, -1):
+            onto = ysolve[2, segments(j)]
+            for i in range(len(lines)):
+                v[i].append(w[i][j] + onto * v[i][-1])
+        rising, falling = [a[0] for a in v], [a[-1] for a in v]
+        for k, d in enumerate((1, 2, 4)):
+            up, back = ysolve[5 + k, segments(seg - 1)], ysolve[8 + k, segments(0)]
+            rising = [a + up * pltpu.roll(a, d, 0) for a in rising]
+            falling = [a + back * pltpu.roll(a, 8 - d, 0) for a in falling]
+        rising, falling = [pltpu.roll(a, 1, 0) for a in rising], [pltpu.roll(a, 7, 0) for a in falling]
+        for j in range(seg):
+            up, back = ysolve[3, segments(j)], ysolve[4, segments(j)]
+            for i, (t, z, _) in enumerate(lines):
+                value = v[i][seg - 1 - j] + (up * rising[i] + back * falling[i])
+                along[t, z, segments(j)] = value
+                if j == 0:
+                    ye[0, t, pl.ds(z, 1)] = value[0:1]
+                if j == seg - 1:
+                    ye[1, t, pl.ds(z, 1)] = value[7:8]
+
     def second_pass(slot, _):
         for p in range(planes):
             z = zc - 1 - (slot * planes + p)
-            falling = ztab[3, pl.ds(z, 1)]
-            for b in range(nt // per):
+            onto = ztab[3, pl.ds(z, 1)]
+            solved = []
+            for b in range(nt // (2 * per)):
                 ready = []
                 for t in range(b * per, (b + 1) * per):
-                    v = base[t, z] + falling * vprev[t]
+                    v = base[t, z] + onto * vprev[t]
                     vprev[t] = v
                     ready.append(v - u[t, z, 8:8 + yc])
-                solved = y_solve(ready)
+                solved.append(y_solve(ready))
+            for g in range(nt // (2 * TOGETHER), nt // TOGETHER):
+                lines = []
+                for t in range(g * TOGETHER, (g + 1) * TOGETHER):
+                    ready = []
+                    for j in range(seg):
+                        v = base[t, z, segments(j)] + onto * vprev[t, j * 8:(j + 1) * 8]
+                        vprev[t, j * 8:(j + 1) * 8] = v
+                        ready.append(v - u[t, z, pl.ds(8 + j, 8, stride=seg)])
+                    lines.append((t, z, ready))
+                y_lines(lines)
+            for b, both in enumerate(solved):
                 for i in range(per):
                     t = b * per + i
-                    part = solved[:, i * LANES:(i + 1) * LANES]
-                    base[t, z] = part
+                    part = both[:, i * LANES:(i + 1) * LANES]
+                    along[t, z] = part
                     ye[0, t, pl.ds(z, 1)] = part[0:1]
                     ye[1, t, pl.ds(z, 1)] = part[yc - 1:yc]
         relays(SECOND_NS * slot, SECOND_NS * (slot + 1))
@@ -500,7 +572,7 @@
     def third(slot):
         zs = [slot * wide + p for p in range(wide)]
         solved = x_solve(
-            lambda t: jnp.concatenate([base[t, z] for z in zs], axis=0), xw, xpass, xthrough, nt
+            lambda t: jnp.concatenate([along[t, z] for z in zs], axis=0), xw, xpass, xthrough, nt
         )
         for t in range(nt):
             for p, z in enumerate(zs):
@@ -685,6 +757,8 @@
             on_chip(2, nt, LANES),
             on_chip(2, nb, LANES),
             on_chip(yc, 3 * yc, dtype=bf16),
+            on_chip(11, yc, LANES),
+            on_chip(nt, zc, yc, LANES),
             on_chip(2, nr, LANES),
             on_chip(nt, yc, LANES),
             on_chip(2, nk, nt, 8, LANES),

time: 37.9 us -> 36.7 us (0.968)
  Pallas kernels: 37.7 us -> 36.5 us
    pallas_call x1, Pallas kernels: 34.2 us -> 32.9 us  [body(): pl.pallas_call(functools.partial(main_kernel, nr, nc, planes, wide, u_ban...]
where the time goes in v4:
time: 36.7 us; the launch traced here: 36.5 us
  Pallas kernels  36.5 us (99%)
    pallas_call x1, Pallas kernels, body(): pl.pallas_call(functools.partial(main_kernel, nr, nc, planes, wide, u_ban...  32.9 us
    pallas_call x1, Pallas kernels, body(): pl.pallas_call(functools.partial(finish_kernel, last), in_specs=[vmem] *...  3.56 us

profile of v4, /device:TPU:0, one launch (start us, length us, event | category | flops | bytes accessed | tf_op | source)
XLA Modules:
  0.0 36.5 jit_solution(18427607563693667915)
XLA Ops:
  0.0 32.9 %shard_map.55 = (f32[8,32,64,128]{3,2,1,0:T(8,128)S(1)}, f32[2,8,32,128]{3,2,1,0:T(8,128)S(1)}, f32[2,8,64,128]{3,2,1,0:T(8,128)S(1)}, f32[2,32,128]{2,1,0:T(8,128)S(1)}, f32[2,64,128]{2,1,0:T(8,128)S(1)}) custom-call(f32[1,1024]{1,0:T(1,128)} %bitcast.3, f32[1,256]{1,0:T(1,128)} %bitcast.4, f32[1,256]{1,0:T(1,128)} %bitcast.5, f32[32,64,1024]{2,1,0:T(8,128)} %field_ref.1, ...), custom_call_target="tpu_custom_call" | custom-call | tf_op jit(solution)/shard_map/pallas_call | solution.py:735
  32.9 3.6 %shard_map.56 = f32[32,64,1024]{2,1,0:T(8,128)} custom-call(f32[8,32,64,128]{3,2,1,0:T(8,128)S(1)} %get-tuple-element.10.base, f32[2,8,32,128]{3,2,1,0:T(8,128)S(1)} %get-tuple-element.11.sy_ref, f32[2,8,64,128]{3,2,1,0:T(8,128)S(1)} %get-tuple-element.12.sz_ref, f32[2,32,128]{2,1,0:T(8,128)S(1)} %get-tuple-element.13.zpass, ...), custom_call_target="tpu_custom_call" | custom-call | tf_op jit(solution)/shard_map/pallas_call | solution.py:783

commit v5 on v4

--- a/solution.py
+++ b/solution.py
@@ -15,7 +15,7 @@
 MAIN_VMEM = 32 * 1024 * 1024
 LAST_VMEM = 12 * 1024 * 1024
 FIRST_NS, HOP_NS, CHUNK_NS = 1100, 2100, 250
-SECOND_NS, TABLE_NS, THIRD_NS = 280, 180, 820
+SECOND_NS, TABLE_NS, THIRD_NS = 330, 150, 1350
 
 
 def shifted(a, by, fill):
@@ -722,7 +722,7 @@
     nb = nx // bx
     u_bands = [16] * (yc // 16) if yc % 16 == 0 else [yc]
     planes = next(p for p in (2, 1) if zc % p == 0)
-    wide = next(p for p in (4, 2, 1) if zc % p == 0)
+    wide = next(p for p in (8, 4, 2, 1) if zc % p == 0)
     length = -(-max(x_faces.shape[0], y_faces.shape[0], z_faces.shape[0]) // LANES) * LANES
     hbm = pl.BlockSpec(memory_space=pltpu.HBM)
     vmem = pl.BlockSpec(memory_space=pltpu.VMEM)

time: 36.7 us -> 36.2 us (0.986); the launches traced: 36.5 us -> 35.6 us
  Pallas kernels: 36.5 us -> 35.6 us
    pallas_call x1, Pallas kernels: 32.9 us -> 32 us  [body(): pl.pallas_call(functools.partial(main_kernel, nr, nc, planes, wide, u_ban...]
where the time goes in v5:
time: 36.2 us; the launch traced here: 35.6 us
  Pallas kernels  35.6 us (98%)
    pallas_call x1, Pallas kernels, body(): pl.pallas_call(functools.partial(main_kernel, nr, nc, planes, wide, u_ban...  32 us
    pallas_call x1, Pallas kernels, body(): pl.pallas_call(functools.partial(finish_kernel, last), in_specs=[vmem] *...  3.56 us

profile of v5, /device:TPU:0, one launch (start us, length us, event | category | flops | bytes accessed | tf_op | source)
XLA Modules:
  0.0 35.6 jit_solution(7866375936897667658)
XLA Ops:
  0.0 32.0 %shard_map.55 = (f32[8,32,64,128]{3,2,1,0:T(8,128)S(1)}, f32[2,8,32,128]{3,2,1,0:T(8,128)S(1)}, f32[2,8,64,128]{3,2,1,0:T(8,128)S(1)}, f32[2,32,128]{2,1,0:T(8,128)S(1)}, f32[2,64,128]{2,1,0:T(8,128)S(1)}) custom-call(f32[1,1024]{1,0:T(1,128)} %bitcast.3, f32[1,256]{1,0:T(1,128)} %bitcast.4, f32[1,256]{1,0:T(1,128)} %bitcast.5, f32[32,64,1024]{2,1,0:T(8,128)} %field_ref.1, ...), custom_call_target="tpu_custom_call" | custom-call | tf_op jit(solution)/shard_map/pallas_call | solution.py:735
  32.0 3.6 %shard_map.56 = f32[32,64,1024]{2,1,0:T(8,128)} custom-call(f32[8,32,64,128]{3,2,1,0:T(8,128)S(1)} %get-tuple-element.10.base, f32[2,8,32,128]{3,2,1,0:T(8,128)S(1)} %get-tuple-element.11.sy_ref, f32[2,8,64,128]{3,2,1,0:T(8,128)S(1)} %get-tuple-element.12.sz_ref, f32[2,32,128]{2,1,0:T(8,128)S(1)} %get-tuple-element.13.zpass, ...), custom_call_target="tpu_custom_call" | custom-call | tf_op jit(solution)/shard_map/pallas_call | solution.py:783

commit v6 on v5

--- a/solution.py
+++ b/solution.py
@@ -368,7 +368,7 @@
     def chunk_at(j):
         return lax.rem(j + 1, nk)
 
-    lag = (5 * far + 1) // 2
+    lag = 3 * far
 
     lane = lax.broadcasted_iota(jnp.int32, (8, LANES), 1)
     group = min(nt, 8)
@@ -504,16 +504,16 @@
             z = zc - 1 - (slot * planes + p)
             onto = ztab[3, pl.ds(z, 1)]
             solved = []
-            for b in range(nt // (2 * per)):
+            for b in range(nt // per - 1):
                 ready = []
                 for t in range(b * per, (b + 1) * per):
                     v = base[t, z] + onto * vprev[t]
                     vprev[t] = v
                     ready.append(v - u[t, z, 8:8 + yc])
                 solved.append(y_solve(ready))
-            for g in range(nt // (2 * TOGETHER), nt // TOGETHER):
+            for g in range(1):
                 lines = []
-                for t in range(g * TOGETHER, (g + 1) * TOGETHER):
+                for t in range(nt - per, nt):
                     ready = []
                     for j in range(seg):
                         v = base[t, z, segments(j)] + onto * vprev[t, j * 8:(j + 1) * 8]

time: 36.2 us -> 36.2 us (level)
  no operation moved by 1% of the time
where the time goes in v6:
time: 36.2 us; the launch traced here: 35.6 us
  Pallas kernels  35.6 us (98%)
    pallas_call x1, Pallas kernels, body(): pl.pallas_call(functools.partial(main_kernel, nr, nc, planes, wide, u_ban...  32 us
    pallas_call x1, Pallas kernels, body(): pl.pallas_call(functools.partial(finish_kernel, last), in_specs=[vmem] *...  3.56 us

profile of v6, /device:TPU:0, one launch (start us, length us, event | category | flops | bytes accessed | tf_op | source)
XLA Modules:
  0.0 35.6 jit_solution(869715099927840450)
XLA Ops:
  0.0 32.0 %shard_map.55 = (f32[8,32,64,128]{3,2,1,0:T(8,128)S(1)}, f32[2,8,32,128]{3,2,1,0:T(8,128)S(1)}, f32[2,8,64,128]{3,2,1,0:T(8,128)S(1)}, f32[2,32,128]{2,1,0:T(8,128)S(1)}, f32[2,64,128]{2,1,0:T(8,128)S(1)}) custom-call(f32[1,1024]{1,0:T(1,128)} %bitcast.3, f32[1,256]{1,0:T(1,128)} %bitcast.4, f32[1,256]{1,0:T(1,128)} %bitcast.5, f32[32,64,1024]{2,1,0:T(8,128)} %field_ref.1, ...), custom_call_target="tpu_custom_call" | custom-call | tf_op jit(solution)/shard_map/pallas_call | solution.py:735
  32.0 3.6 %shard_map.56 = f32[32,64,1024]{2,1,0:T(8,128)} custom-call(f32[8,32,64,128]{3,2,1,0:T(8,128)S(1)} %get-tuple-element.10.base, f32[2,8,32,128]{3,2,1,0:T(8,128)S(1)} %get-tuple-element.11.sy_ref, f32[2,8,64,128]{3,2,1,0:T(8,128)S(1)} %get-tuple-element.12.sz_ref, f32[2,32,128]{2,1,0:T(8,128)S(1)} %get-tuple-element.13.zpass, ...), custom_call_target="tpu_custom_call" | custom-call | tf_op jit(solution)/shard_map/pallas_call | solution.py:783
